TPU v7x, 32 devices: a whole 2x2x4 slice. The times are simulated.
32 devices in a mesh: seq: 16 (over z, y, x), chan: 2 (over core).
Axes of the slice: x: 2, y: 2, z: 4, core: 2. Of those that a mesh axis runs over, the one named last changes fastest.
Arguments:
- values: bfloat16 [256, 8192], P('chan', 'seq'), may hold values from -6 to 6
- gate_one: bfloat16 [256, 8192], P('chan', 'seq'), may hold values from -6 to 6
- gate_two: bfloat16 [256, 8192], P('chan', 'seq'), may hold values from -6 to 6
- filter_one: float32 [256, 8192], P('chan', 'seq'), may hold values from -1 to 1
- filter_two: float32 [256, 8192], P('chan', 'seq'), may hold values from -1 to 1
- skip_one: float32 [256], P('chan'), may hold values from -1 to 1
- skip_two: float32 [256], P('chan'), may hold values from -1 to 1
- mix_weight: bfloat16 [256, 256], P(None, 'chan'), may hold values from -0.375 to 0.375
Outputs:
- mixed: bfloat16 [256, 8192], P('chan', 'seq')
All inputs are finite; a program needn't handle non-finite values.
Results may differ from a plain program's by a relative error of at most 0.0051.
Values may be sent and summed in bfloat16 or wider, within the bound.
A program may use at most 64 MiB of HBM per device.

v0:
```python
import math

import jax
import jax.numpy as jnp
from jax import lax
from jax.sharding import PartitionSpec as P

FOLD = 512


exact_mode = lax.Precision.HIGHEST


def angle_of(integers, modulus):
    return integers.astype(jnp.float32) * (2.0 * math.pi / modulus)


def fourier_rows(half_rows, column_count, period):
    row_index = lax.iota(jnp.int32, half_rows)[:, None]
    column_index = lax.iota(jnp.int32, column_count)[None, :]
    angles = angle_of(row_index * column_index % period, period)
    cosine = jnp.cos(angles)
    sine_tab = jnp.sin(angles)
    alternate = (1 - 2 * (row_index % 2)).astype(jnp.float32)
    sine_tab = jnp.where(column_index == 0, -alternate, sine_tab)
    return (cosine, sine_tab)


def fold_tables():
    points = lax.iota(jnp.int32, FOLD)
    angles = angle_of(points[:, None] * points[None, :] % FOLD, FOLD)
    return (jnp.cos(angles), jnp.sin(angles))


def spectra(columns_in):
    narrow = columns_in.shape[1]
    half_rows = columns_in.shape[2]
    period = 2 * half_rows
    modulus = period * FOLD
    seq_index = lax.axis_index("seq")
    cosine, sine_tab = fourier_rows(half_rows, half_rows, period)
    real_part = jnp.einsum("kra,ac->krc", columns_in, cosine, precision=exact_mode)
    imag_part = -jnp.einsum("kra,ac->krc", columns_in, sine_tab, precision=exact_mode)
    points_glob = seq_index * narrow + lax.iota(jnp.int32, narrow)
    column_index = lax.iota(jnp.int32, cosine.shape[1])
    angles = angle_of(points_glob[:, None] * column_index[None, :] % modulus, modulus)
    turn_cos = jnp.cos(angles)
    turn_sin = jnp.sin(angles)
    real_twist = real_part * turn_cos + imag_part * turn_sin
    imag_twist = imag_part * turn_cos - real_part * turn_sin
    real_recv, imag_recv = (
        lax.all_to_all(real_twist, "seq", split_axis=2, concat_axis=1, tiled=True),
        lax.all_to_all(imag_twist, "seq", split_axis=2, concat_axis=1, tiled=True),
    )
    row_count = real_recv.shape[2]
    is_leader = seq_index == 0
    spare_row = imag_recv
    phases = angle_of(lax.iota(jnp.int32, FOLD), 2 * FOLD)[None, :, None]
    row_mask = ((lax.iota(jnp.int32, row_count) == 0) & is_leader)[None, None, :]
    imag_recv = jnp.where(row_mask, 0.0, imag_recv)
    real_recv = jnp.concatenate([real_recv, spare_row * jnp.cos(phases)], axis=2)
    imag_recv = jnp.concatenate([imag_recv, -spare_row * jnp.sin(phases)], axis=2)
    rows_glob = jnp.concatenate(
        [
            seq_index * row_count + lax.iota(jnp.int32, row_count),
            jnp.full((1,), half_rows, jnp.int32),
        ]
    )
    cosine_q, sine_q = fold_tables()
    first_prod = jnp.einsum("kbr,bd->krd", real_recv + imag_recv, cosine_q, precision=exact_mode)
    second_prod = jnp.einsum("kbr,bd->krd", real_recv, -sine_q - cosine_q, precision=exact_mode)
    third_prod = jnp.einsum("kbr,bd->krd", imag_recv, cosine_q - sine_q, precision=exact_mode)
    return (first_prod - third_prod, first_prod + second_prod, rows_glob)


def inverse(spec_real, spectrum_imaginary, rows_glob, half_rows):
    period = 2 * half_rows
    modulus = period * FOLD
    seq_index = lax.axis_index("seq")
    cosine_q, sine_q = fold_tables()
    first_prod = jnp.einsum(
        "krd,db->kbr", spec_real + spectrum_imaginary, cosine_q, precision=exact_mode
    )
    second_prod = jnp.einsum("krd,db->kbr", spec_real, sine_q - cosine_q, precision=exact_mode)
    third_prod = jnp.einsum(
        "krd,db->kbr", spectrum_imaginary, cosine_q + sine_q, precision=exact_mode
    )
    real_part = first_prod - third_prod
    imag_part = first_prod + second_prod
    angles = angle_of(lax.iota(jnp.int32, FOLD)[:, None] * rows_glob[None, :] % modulus, modulus)
    turn_cos = jnp.cos(angles)
    turn_sin = jnp.sin(angles)
    real_twist = real_part * turn_cos - imag_part * turn_sin
    imag_twist = real_part * turn_sin + imag_part * turn_cos
    row_count = real_twist.shape[2] - 1
    row_mask = ((lax.iota(jnp.int32, row_count) == 0) & (seq_index == 0))[None, None, :]
    imag_send = jnp.where(row_mask, real_twist[:, :, row_count:], imag_twist[:, :, :row_count])
    real_recv, imag_recv = (
        lax.all_to_all(
            real_twist[:, :, :row_count], "seq", split_axis=1, concat_axis=2, tiled=True
        ),
        lax.all_to_all(imag_send, "seq", split_axis=1, concat_axis=2, tiled=True),
    )
    cosine, sine_tab = fourier_rows(half_rows, half_rows, period)
    coefficient_matrix = jnp.where(lax.iota(jnp.int32, half_rows) == 0, 1.0, 2.0).astype(
        jnp.float32
    )[None, :]
    cosine = cosine * coefficient_matrix
    sine_tab = sine_tab * coefficient_matrix
    result = jnp.einsum("kbc,ac->kba", real_recv, cosine, precision=exact_mode)
    result = result - jnp.einsum("kbc,ac->kba", imag_recv, sine_tab, precision=exact_mode)
    return result / modulus


def convolve(value_real, value_imag, filter_real, filter_imag, rows_glob, half_rows):
    prod_real = value_real * filter_real - value_imag * filter_imag
    prod_imag = value_real * filter_imag + value_imag * filter_real
    return inverse(prod_real, prod_imag, rows_glob, half_rows)


def per_device(values, gate_one, gate_two, filter_one, filter_two, skip_one, skip_two, mix_weight):
    channels, tokens = values.shape
    blocks = tokens // FOLD

    def columns(source):
        return jnp.swapaxes(source.reshape(channels, blocks, FOLD), 1, 2)

    def from_columns(result_cols):
        return jnp.swapaxes(result_cols, 1, 2).reshape(channels, tokens)

    def to_tokens(result_cols):
        return from_columns(
            lax.all_to_all(result_cols, "seq", split_axis=2, concat_axis=1, tiled=True)
        )

    values_cols = lax.all_to_all(columns(values), "seq", split_axis=1, concat_axis=2, tiled=True)
    filter_cols = (
        lax.all_to_all(columns(filter_one), "seq", split_axis=1, concat_axis=2, tiled=True),
        lax.all_to_all(columns(filter_two), "seq", split_axis=1, concat_axis=2, tiled=True),
    )
    values_wide = values_cols.astype(jnp.float32)
    half_rows = values_wide.shape[2]
    stacked = jnp.concatenate([values_wide, filter_cols[0], filter_cols[1]], axis=0)
    spec_real, spectrum_imaginary, rows_glob = spectra(stacked)
    conv_one = convolve(
        spec_real[:channels],
        spectrum_imaginary[:channels],
        spec_real[channels : 2 * channels],
        spectrum_imaginary[channels : 2 * channels],
        rows_glob,
        half_rows,
    )
    filter_two_real = spec_real[2 * channels :]
    filter_two_imag = spectrum_imaginary[2 * channels :]
    conv_tokens = to_tokens(conv_one)
    gated = gate_one.astype(jnp.float32) * (
        conv_tokens + skip_one[:, None] * values.astype(jnp.float32)
    )
    gated_cols = lax.all_to_all(columns(gated), "seq", split_axis=1, concat_axis=2, tiled=True)
    second_real, second_imag, restored_lines = spectra(gated_cols)
    conv_two = convolve(
        second_real, second_imag, filter_two_real, filter_two_imag, restored_lines, half_rows
    )
    second_tokens = to_tokens(conv_two)
    mixed_in = (gate_two.astype(jnp.float32) * (second_tokens + skip_two[:, None] * gated)).astype(
        jnp.bfloat16
    )
    summed = jnp.einsum(
        "de,dt->et",
        mix_weight,
        lax.all_gather(mixed_in, "chan", axis=0, tiled=True),
        preferred_element_type=jnp.float32,
    )
    return jax.nn.silu(summed).astype(jnp.bfloat16)


def solution(mesh):
    return jax.shard_map(
        per_device,
        mesh=mesh,
        in_specs=(
            P("chan", "seq"),
            P("chan", "seq"),
            P("chan", "seq"),
            P("chan", "seq"),
            P("chan", "seq"),
            P("chan"),
            P("chan"),
            P(None, "chan"),
        ),
        out_specs=P("chan", "seq"),
        check_vma=False,
    )
```

profile of v0, /device:TPU:0, one launch (start us, length us, event | category | flops | bytes accessed | tf_op | source)
XLA Modules:
  0.0 290.8 jit_solution(13032931578427769664)
XLA Ops:
  3.7 8.3 %all-to-all-start = ((bf16[16,2,2048]{2,1,0:T(2,128)(2,1)}), bf16[16,2,2048]{2,1,0:T(2,128)(2,1)S(1)}, u32[]{:S(2)}, u32[]{:S(2)}) async-start(bf16[16,2,2048]{2,1,0:T(2,128)(2,1)} %reshape.345), calls=%async_computation | async-start | bytes 262144 | tf_op jit(solution)/shard_map/all_to_all | solution.py:136
  13.9 6.0 %all-to-all-done = bf16[16,2,2048]{2,1,0:T(2,128)(2,1)S(1)} async-done(((bf16[16,2,2048]{2,1,0:T(2,128)(2,1)}), bf16[16,2,2048]{2,1,0:T(2,128)(2,1)S(1)}, u32[]{:S(2)}, u32[]{:S(2)}) %all-to-all-start) | async-done | bytes 131104 | tf_op jit(solution)/shard_map/all_to_all | solution.py:136
  24.3 7.6 %all-to-all-done.2 = f32[128,512,1]{0,2,1:T(1,128)S(1)} async-done(((f32[128,512,1]{0,2,1:T(1,128)}), f32[128,512,1]{0,2,1:T(1,128)S(1)}, u32[]{:S(2)}, u32[]{:S(2)}) %all-to-all-start.2) | async-done | bytes 262176 | tf_op jit(solution)/shard_map/all_to_all | solution.py:139
  36.2 8.4 %all-to-all-done.1 = f32[128,512,1]{0,2,1:T(1,128)S(1)} async-done(((f32[128,512,1]{0,2,1:T(1,128)}), f32[128,512,1]{0,2,1:T(1,128)S(1)}, u32[]{:S(2)}, u32[]{:S(2)}) %all-to-all-start.1) | async-done | bytes 262176 | tf_op jit(solution)/shard_map/all_to_all | solution.py:138
  52.6 17.7 %all-to-all-done.4 = f32[384,32,16]{0,1,2:T(8,128)S(1)} async-done(((f32[384,32,16]{0,1,2:T(8,128)}), f32[384,32,16]{0,1,2:T(8,128)S(1)}, u32[]{:S(2)}, u32[]{:S(2)}) %all-to-all-start.4) | async-done | bytes 786464 | tf_op jit(solution)/shard_map/all_to_all | solution.py:53
  70.4 5.4 %all-to-all-start.3 = ((f32[384,32,16]{0,1,2:T(8,128)}), f32[384,32,16]{0,1,2:T(8,128)S(1)}, u32[]{:S(2)}, u32[]{:S(2)}) async-start(f32[384,32,16]{0,1,2:T(8,128)} %copy.118), calls=%async_computation.3 | async-start | bytes 1572864 | tf_op jit(solution)/shard_map/all_to_all | solution.py:52
  76.3 17.6 %all-to-all-done.3 = f32[384,32,16]{0,1,2:T(8,128)S(1)} async-done(((f32[384,32,16]{0,1,2:T(8,128)}), f32[384,32,16]{0,1,2:T(8,128)S(1)}, u32[]{:S(2)}, u32[]{:S(2)}) %all-to-all-start.3) | async-done | bytes 786464 | tf_op jit(solution)/shard_map/all_to_all | solution.py:52
  94.5 6.5 %fusion = f32[384,2,512]{2,0,1:T(8,128)S(1)} fusion(f32[384,512,1]{1,0,2:T(8,128)S(1)} %get-tuple-element.16, f32[384,512,1]{1,0,2:T(8,128)S(1)} %get-tuple-element.17, f32[384,512,1]{1,0,2:T(8,128)S(1)} %get-tuple-element.15, f32[384,512,1]{1,0,2:T(8,128)S(1)} %copy.121), kind=kOutput, calls=%fused_computation.2 | convolution fusion | flops 2420768768 | bytes 4718592 | tf_op jit(solution)/shard_map/kbr,bd->krd/dot_general | solution.py:70
  101.0 7.0 %convolution_subtract_fusion = f32[384,2,512]{2,0,1:T(8,128)S(1)} fusion(f32[384,2,512]{2,0,1:T(8,128)S(1)} %fusion, f32[384,512,1]{1,0,2:T(8,128)S(1)} %get-tuple-element.16, f32[384,512,1]{1,0,2:T(8,128)S(1)} %get-tuple-element.17), kind=kOutput, calls=%fused_computation.8 | convolution fusion | flops 2420637696 | bytes 4718592 | tf_op jit(solution)/shard_map/kbr,bd->krd/dot_general | solution.py:72
  108.1 6.9 %convolution_add_fusion = f32[384,2,512]{2,0,1:T(8,128)S(1)} fusion(f32[384,2,512]{2,0,1:T(8,128)S(1)} %fusion, f32[384,512,1]{1,0,2:T(8,128)S(1)} %get-tuple-element.15, f32[384,512,1]{1,0,2:T(8,128)S(1)} %copy.121), kind=kOutput, calls=%fused_computation.7 | convolution fusion | flops 2420899840 | bytes 4718592 | tf_op jit(solution)/shard_map/kbr,bd->krd/dot_general | solution.py:71
  126.5 6.0 %add_bitcast_fusion.1 = (f32[128,512,2]{0,1,2:T(8,128)S(1)}, f32[128,512,2]{0,1,2:T(8,128)S(1)}) fusion(f32[512,128,2]{1,0,2:T(8,128)S(1)} %convolution_add_fusion.3, f32[512,2]{0,1:T(2,128)S(1)} %get-tuple-element.28, f32[512,2]{0,1:T(2,128)S(1)} %get-tuple-element.27, f32[512,128,2]{1,0,2:T(8,128)S(1)} %fusion.20, f32[128,2,512]{2,0,1:T(8,128)S(1)} %get-tuple-element.7), kind=kOutput, calls=%fused_computation.57 | convolution fusion | flops 810156032 | bytes 2629632 | tf_op jit(solution)/shard_map/krd,db->kbr/dot_general | solution.py:85
  133.3 13.2 %all_to_all.237 = f32[128,512,1]{0,2,1:T(1,128)S(1)} all-to-all(f32[128,512,1]{0,2,1:T(1,128)S(1)} %bitcast.205), channel_id=1, replica_groups=mesh['seq'=16,'chan'=2] {'seq'}, dimensions={1} | all-to-all | bytes 524288 | tf_op jit(solution)/shard_map/all_to_all | solution.py:99
  151.1 8.4 %all-to-all-done.6 = f32[128,512,1]{0,2,1:T(1,128)S(1)} async-done(((f32[128,512,1]{0,2,1:T(1,128)}), f32[128,512,1]{0,2,1:T(1,128)S(1)}, u32[]{:S(2)}, u32[]{:S(2)}) %all-to-all-start.6) | async-done | bytes 262176 | tf_op jit(solution)/shard_map/all_to_all | solution.py:102
  164.6 8.8 %all-to-all-done.7 = f32[128,32,16]{0,1,2:T(8,128)S(1)} async-done(((f32[128,32,16]{0,1,2:T(8,128)}), f32[128,32,16]{0,1,2:T(8,128)S(1)}, u32[]{:S(2)}, u32[]{:S(2)}) %all-to-all-start.7) | async-done | bytes 262176 | tf_op jit(solution)/shard_map/all_to_all | solution.py:133
  173.5 12.4 %all_to_all.238 = f32[128,512,1]{0,2,1:T(1,128)S(1)} all-to-all(f32[128,512,1]{0,2,1:T(1,128)S(1)} %bitcast.203), channel_id=1, replica_groups=mesh['seq'=16,'chan'=2] {'seq'}, dimensions={1} | all-to-all | bytes 524288 | tf_op jit(solution)/shard_map/all_to_all | solution.py:159
  192.3 8.3 %all-to-all-done.10 = f32[128,32,16]{0,1,2:T(8,128)S(1)} async-done(((f32[128,32,16]{0,1,2:T(8,128)}), f32[128,32,16]{0,1,2:T(8,128)S(1)}, u32[]{:S(2)}, u32[]{:S(2)}) %all-to-all-start.10) | async-done | bytes 262176 | tf_op jit(solution)/shard_map/all_to_all | solution.py:53
  204.3 8.9 %all-to-all-done.9 = f32[128,32,16]{0,1,2:T(8,128)S(1)} async-done(((f32[128,32,16]{0,1,2:T(8,128)}), f32[128,32,16]{0,1,2:T(8,128)S(1)}, u32[]{:S(2)}, u32[]{:S(2)}) %all-to-all-start.9) | async-done | bytes 262176 | tf_op jit(solution)/shard_map/all_to_all | solution.py:52
  213.2 5.6 %fusion.15 = f32[128,2,512]{2,0,1:T(8,128)S(1)} fusion(f32[128,512,1]{0,1,2:T(8,128)S(1)} %get-tuple-element.26, f32[128,512,1]{0,1,2:T(8,128)S(1)} %get-tuple-element.25, f32[128,512,1]{0,1,2:T(8,128)S(1)} %get-tuple-element.24, f32[128,512,1]{0,1,2:T(8,128)S(1)} %bitcast.217), kind=kOutput, calls=%fused_computation.33 | convolution fusion | flops 809369600 | bytes 1572864 | tf_op jit(solution)/shard_map/kbr,bd->krd/dot_general | solution.py:70
  218.8 6.3 %convolution_subtract_fusion.2 = f32[128,2,512]{2,0,1:T(8,128)S(1)} fusion(f32[128,2,512]{2,0,1:T(8,128)S(1)} %fusion.15, f32[128,512,1]{0,1,2:T(8,128)S(1)} %get-tuple-element.26, f32[128,512,1]{0,1,2:T(8,128)S(1)} %get-tuple-element.25), kind=kOutput, calls=%fused_computation.13 | convolution fusion | flops 809500672 | bytes 1572864 | tf_op jit(solution)/shard_map/kbr,bd->krd/dot_general | solution.py:72
  225.1 7.1 %multiply_add_fusion.1 = (f32[128,2,512]{2,0,1:T(8,128)S(1)}, f32[128,2,512]{2,0,1:T(8,128)S(1)}) fusion(f32[128,2,512]{2,0,1:T(8,128)S(1)} %convolution_subtract_fusion.2, f32[384,2,512]{2,0,1:T(8,128)} %copy-done.1, f32[384,2,512]{2,0,1:T(8,128)S(1)} %convolution_subtract_fusion, f32[128,2,512]{2,0,1:T(8,128)S(1)} %fusion.15, ...), kind=kOutput, calls=%fused_computation.54 | convolution fusion | flops 810549248 | bytes 3670016 | tf_op jit(solution)/shard_map/kbr,bd->krd/dot_general | solution.py:71
  237.1 5.3 %convolution_add_fusion.1 = f32[512,128,2]{1,0,2:T(8,128)S(1)} fusion(f32[512,128,2]{1,0,2:T(8,128)S(1)} %fusion.18, f32[128,2,512]{2,0,1:T(8,128)S(1)} %get-tuple-element.6), kind=kOutput, calls=%fused_computation.10 | convolution fusion | flops 809369600 | bytes 1572864 | tf_op jit(solution)/shard_map/krd,db->kbr/dot_general | solution.py:84
  248.4 12.4 %all_to_all.239 = f32[128,512,1]{0,2,1:T(1,128)S(1)} all-to-all(f32[128,512,1]{0,2,1:T(1,128)S(1)} %bitcast.204), channel_id=1, replica_groups=mesh['seq'=16,'chan'=2] {'seq'}, dimensions={1} | all-to-all | bytes 524288 | tf_op jit(solution)/shard_map/all_to_all | solution.py:99
  265.0 8.5 %all-to-all-done.12 = f32[128,512,1]{0,2,1:T(1,128)S(1)} async-done(((f32[128,512,1]{0,2,1:T(1,128)}), f32[128,512,1]{0,2,1:T(1,128)S(1)}, u32[]{:S(2)}, u32[]{:S(2)}) %all-to-all-start.12) | async-done | bytes 262176 | tf_op jit(solution)/shard_map/all_to_all | solution.py:102
  278.6 8.9 %all-to-all-done.13 = f32[128,32,16]{0,1,2:T(8,128)S(1)} async-done(((f32[128,32,16]{0,1,2:T(8,128)}), f32[128,32,16]{0,1,2:T(8,128)S(1)}, u32[]{:S(2)}, u32[]{:S(2)}) %all-to-all-start.13) | async-done | bytes 262176 | tf_op jit(solution)/shard_map/all_to_all | solution.py:133
  (77 shorter events, 78.2 us)
Async XLA Ops:
  0.0 289.6 %copy-start = (bf16[256,128]{1,0:T(8,128)(2,1)S(1)}, bf16[256,128]{1,0:T(8,128)(2,1)}, u32[]{:S(2)}) copy-start(bf16[256,128]{1,0:T(8,128)(2,1)} %param.15) | copy-start | bytes 196612
  0.0 23.4 %copy-start.3 = (f32[128,512]{1,0:T(8,128)S(1)}, f32[128,512]{1,0:T(8,128)}, u32[]{:S(2)}) copy-start(f32[128,512]{1,0:T(8,128)} %param.11) | copy-start | bytes 786436
  3.7 16.1 %all-to-all-start = ((bf16[16,2,2048]{2,1,0:T(2,128)(2,1)}), bf16[16,2,2048]{2,1,0:T(2,128)(2,1)S(1)}, u32[]{:S(2)}, u32[]{:S(2)}) async-start(bf16[16,2,2048]{2,1,0:T(2,128)(2,1)} %reshape.345), calls=%async_computation | async-start | bytes 262144 | tf_op jit(solution)/shard_map/all_to_all | solution.py:136
  19.9 12.0 %all-to-all-start.2 = ((f32[128,512,1]{0,2,1:T(1,128)}), f32[128,512,1]{0,2,1:T(1,128)S(1)}, u32[]{:S(2)}, u32[]{:S(2)}) async-start(f32[128,512,1]{0,2,1:T(1,128)} %bitcast.9), calls=%async_computation.2 | async-start | bytes 524288 | tf_op jit(solution)/shard_map/all_to_all | solution.py:139
  31.9 12.7 %all-to-all-start.1 = ((f32[128,512,1]{0,2,1:T(1,128)}), f32[128,512,1]{0,2,1:T(1,128)S(1)}, u32[]{:S(2)}, u32[]{:S(2)}) async-start(f32[128,512,1]{0,2,1:T(1,128)} %bitcast.5), calls=%async_computation.1 | async-start | bytes 524288 | tf_op jit(solution)/shard_map/all_to_all | solution.py:138
  47.9 22.5 %all-to-all-start.4 = ((f32[384,32,16]{0,1,2:T(8,128)}), f32[384,32,16]{0,1,2:T(8,128)S(1)}, u32[]{:S(2)}, u32[]{:S(2)}) async-start(f32[384,32,16]{0,1,2:T(8,128)} %copy.119), calls=%async_computation.4 | async-start | bytes 1572864 | tf_op jit(solution)/shard_map/all_to_all | solution.py:53
  70.4 23.6 %all-to-all-start.3 = ((f32[384,32,16]{0,1,2:T(8,128)}), f32[384,32,16]{0,1,2:T(8,128)S(1)}, u32[]{:S(2)}, u32[]{:S(2)}) async-start(f32[384,32,16]{0,1,2:T(8,128)} %copy.118), calls=%async_computation.3 | async-start | bytes 1572864 | tf_op jit(solution)/shard_map/all_to_all | solution.py:52
  114.9 1.2 copy-start.1
  146.6 17.8 %copy-start.2 = (bf16[128,512]{1,0:T(8,128)(2,1)S(1)}, bf16[128,512]{1,0:T(8,128)(2,1)}, u32[]{:S(2)}) copy-start(bf16[128,512]{1,0:T(8,128)(2,1)} %param.8) | copy-start | bytes 393220
  146.6 17.9 %copy-start.4 = (bf16[128,512]{1,0:T(8,128)(2,1)S(1)}, bf16[128,512]{1,0:T(8,128)(2,1)}, u32[]{:S(2)}) copy-start(bf16[128,512]{1,0:T(8,128)(2,1)} %param.9) | copy-start | bytes 393220
  146.6 12.9 %all-to-all-start.6 = ((f32[128,512,1]{0,2,1:T(1,128)}), f32[128,512,1]{0,2,1:T(1,128)S(1)}, u32[]{:S(2)}, u32[]{:S(2)}) async-start(f32[128,512,1]{0,2,1:T(1,128)} %bitcast.36), calls=%async_computation.6 | async-start | bytes 524288 | tf_op jit(solution)/shard_map/all_to_all | solution.py:102
  150.5 23.0 %copy-start.6 = (f32[128]{0:T(128)S(1)}, f32[128]{0:T(128)}, u32[]{:S(2)}) copy-start(f32[128]{0:T(128)} %param.13) | copy-start | bytes 1540
  160.8 12.7 %all-to-all-start.7 = ((f32[128,32,16]{0,1,2:T(8,128)}), f32[128,32,16]{0,1,2:T(8,128)S(1)}, u32[]{:S(2)}, u32[]{:S(2)}) async-start(f32[128,32,16]{0,1,2:T(8,128)} %copy.131), calls=%async_computation.7 | async-start | bytes 524288 | tf_op jit(solution)/shard_map/all_to_all | solution.py:133
  187.9 12.6 %all-to-all-start.10 = ((f32[128,32,16]{0,1,2:T(8,128)}), f32[128,32,16]{0,1,2:T(8,128)S(1)}, u32[]{:S(2)}, u32[]{:S(2)}) async-start(f32[128,32,16]{0,1,2:T(8,128)} %copy.138), calls=%async_computation.10 | async-start | bytes 524288 | tf_op jit(solution)/shard_map/all_to_all | solution.py:53
  200.6 12.6 %all-to-all-start.9 = ((f32[128,32,16]{0,1,2:T(8,128)}), f32[128,32,16]{0,1,2:T(8,128)S(1)}, u32[]{:S(2)}, u32[]{:S(2)}) async-start(f32[128,32,16]{0,1,2:T(8,128)} %copy.137), calls=%async_computation.9 | async-start | bytes 524288 | tf_op jit(solution)/shard_map/all_to_all | solution.py:52
  260.8 17.7 %copy-start.5 = (bf16[128,512]{1,0:T(8,128)(2,1)S(1)}, bf16[128,512]{1,0:T(8,128)(2,1)}, u32[]{:S(2)}) copy-start(bf16[128,512]{1,0:T(8,128)(2,1)} %param.10) | copy-start | bytes 393220
  260.8 26.7 %copy-start.7 = (f32[128]{0:T(128)S(1)}, f32[128]{0:T(128)}, u32[]{:S(2)}) copy-start(f32[128]{0:T(128)} %param.14) | copy-start | bytes 1540
  260.8 12.8 %all-to-all-start.12 = ((f32[128,512,1]{0,2,1:T(1,128)}), f32[128,512,1]{0,2,1:T(1,128)S(1)}, u32[]{:S(2)}, u32[]{:S(2)}) async-start(f32[128,512,1]{0,2,1:T(1,128)} %bitcast.69), calls=%async_computation.12 | async-start | bytes 524288 | tf_op jit(solution)/shard_map/all_to_all | solution.py:102
  274.9 12.6 %all-to-all-start.13 = ((f32[128,32,16]{0,1,2:T(8,128)}), f32[128,32,16]{0,1,2:T(8,128)S(1)}, u32[]{:S(2)}, u32[]{:S(2)}) async-start(f32[128,32,16]{0,1,2:T(8,128)} %copy.149), calls=%async_computation.13 | async-start | bytes 524288 | tf_op jit(solution)/shard_map/all_to_all | solution.py:133
where the time goes:
time: 296 us; the launch traced here: 291 us
  waiting for transfers between devices  109 us (37%)
  matrix products  76.7 us (26%)
  starting transfers between devices  46.4 us (16%)
  blocking collectives  40.1 us (14%)
  local copies, waits for them, and re-layouts  13.5 us (5%)
  other arithmetic  4.12 us (1%)
    all_to_all x2, waiting for transfers between devices, spectra(): lax.all_to_all(real_twist, 'seq', split_axis=2, concat_axis=1, tiled=True)  26.5 us
    all_to_all x2, waiting for transfers between devices, spectra(): lax.all_to_all(imag_twist, 'seq', split_axis=2, concat_axis=1, tiled=True)  26 us
    all_to_all x2, blocking collectives, inverse(): lax.all_to_all(real_twist[:, :, :row_count], 'seq', split_axis=1, concat_...  25.7 us
    all_to_all x2, waiting for transfers between devices, to_tokens(): lax.all_to_all(result_cols, 'seq', split_axis=2, concat_axis=1, tiled=True)  17.8 us
    all_to_all x2, waiting for transfers between devices, inverse(): lax.all_to_all(imag_send, 'seq', split_axis=1, concat_axis=2, tiled=True)  17 us
    dot_general x2, matrix products, spectra(): jnp.einsum('kbr,bd->krd', real_recv, -sine_q - cosine_q, precision=exact_...  14 us
    dot_general x2, matrix products, spectra(): jnp.einsum('kbr,bd->krd', imag_recv, cosine_q - sine_q, precision=exact_m...  13.3 us
    all_to_all x1, blocking collectives, per_device(): lax.all_to_all(columns(gated), 'seq', split_axis=1, concat_axis=2, tiled=...  12.4 us
  transfers between devices with their start and end apart: 11, of which 11 were waited for; matrix products, arithmetic and copies ran while one was open for 2% of the time, Pallas kernels for 0%

commit v1 on v0

v1 whole, which is shorter than its diff:
```python
import functools

import jax
import jax.numpy as jnp
from jax import lax
from jax.experimental import pallas as pl
from jax.experimental.pallas import tpu as pltpu
from jax.sharding import PartitionSpec as P

LANES = 128
GROUP = 8


def toeplitz_conv(padded, taps, lags):
    row = lax.broadcasted_iota(jnp.int32, (LANES, LANES), 0)
    lane = lax.broadcasted_iota(jnp.int32, (LANES, LANES), 1)
    lower = lane >= row

    def step(group, carry):
        total, before = carry
        left, right = [], []
        for inner in range(GROUP):
            lag = group * GROUP + inner
            line = jnp.broadcast_to(taps[pl.ds(lag, 1), :], (LANES, LANES))
            turned = pltpu.roll(line, 0, 1, stride=1, stride_axis=0)
            right.append(jnp.where(lower, turned, before).astype(jnp.bfloat16))
            before = turned
            left.append(padded[pl.ds(lags - lag, lags), :].astype(jnp.bfloat16))
        total = total + jnp.dot(
            jnp.concatenate(left, axis=1),
            jnp.concatenate(right, axis=0),
            preferred_element_type=jnp.float32,
        )
        return total, before

    start = (jnp.zeros((lags, LANES), jnp.float32), jnp.zeros((LANES, LANES), jnp.float32))
    return lax.fori_loop(0, lags // GROUP, step, start)[0]


def conv_kernel(lags, values, gate, one, two, out, padded):
    padded[pl.ds(0, lags), :] = jnp.zeros((lags, LANES), jnp.float32)
    padded[pl.ds(lags, lags), :] = values[0].astype(jnp.float32)
    first = toeplitz_conv(padded, one.at[0], lags)
    padded[pl.ds(lags, lags), :] = gate[0].astype(jnp.float32) * first
    out[0] = toeplitz_conv(padded, two.at[0], lags).astype(out.dtype)


def both_convs(values, gate, one, two):
    count, lags, _ = values.shape
    block = pl.BlockSpec((1, lags, LANES), lambda c: (c, 0, 0))
    return pl.pallas_call(
        functools.partial(conv_kernel, lags),
        grid=(count,),
        in_specs=[block] * 4,
        out_specs=block,
        out_shape=jax.ShapeDtypeStruct(values.shape, jnp.bfloat16),
        scratch_shapes=[pltpu.VMEM((2 * lags, LANES), jnp.float32)],
    )(values, gate, one, two)


def per_device(seq, values, gate_one, gate_two, filter_one, filter_two, skip_one, skip_two, mix_weight):
    channels, tokens = values.shape
    each = -(-channels // seq)
    first_tap = (lax.iota(jnp.int32, tokens) == 0) & (lax.axis_index("seq") == 0)

    def with_skip(taps, skip):
        return (taps + jnp.where(first_tap[None, :], skip[:, None], 0.0)).astype(jnp.bfloat16)

    def spread(source):
        padded = jnp.pad(source, ((0, each * seq - channels), (0, 0)))
        return padded.reshape(seq, each, tokens)

    sent = jnp.stack(
        [
            spread(values),
            spread(gate_one),
            spread(with_skip(filter_one, skip_one)),
            spread(with_skip(filter_two, skip_two)),
        ],
        axis=1,
    )
    got = lax.all_to_all(sent, "seq", split_axis=0, concat_axis=0, tiled=True)
    lines = jnp.transpose(got, (1, 2, 0, 3)).reshape(4, each, seq * tokens // LANES, LANES)
    conv = both_convs(
        lines[0], lines[1], lines[2].astype(jnp.float32), lines[3].astype(jnp.float32)
    )
    back = jnp.transpose(conv.reshape(each, seq, tokens), (1, 0, 2))
    back = lax.all_to_all(back, "seq", split_axis=0, concat_axis=0, tiled=True)
    back = back.reshape(each * seq, tokens)[:channels]
    mixed_in = (gate_two.astype(jnp.float32) * back.astype(jnp.float32)).astype(jnp.bfloat16)
    summed = jnp.einsum(
        "de,dt->et",
        mix_weight,
        lax.all_gather(mixed_in, "chan", axis=0, tiled=True),
        preferred_element_type=jnp.float32,
    )
    return jax.nn.silu(summed).astype(jnp.bfloat16)


def solution(mesh):
    both = P("chan", "seq")
    return jax.shard_map(
        functools.partial(per_device, mesh.shape["seq"]),
        mesh=mesh,
        in_specs=(both, both, both, both, both, P("chan"), P("chan"), P(None, "chan")),
        out_specs=both,
        check_vma=False,
    )
```

time: 296 us -> 85.3 us (0.29); the launches traced: 291 us -> 85 us
  waiting for transfers between devices: 109 us -> 0 us
  matrix products: 76.7 us -> 0.29 us
  starting transfers between devices: 46.4 us -> 0 us
  Pallas kernels: 0 us -> 40.5 us
  local copies, waits for them, and re-layouts: 13.5 us -> 5.85 us
  blocking collectives: 40.1 us -> 36.9 us
    all_to_all x11 -> x0, waiting for transfers between devices: 109 us -> none  [the longest x2 26.5 us: spectra(): lax.all_to_all(real_twist, 'seq', split_axis=2, concat_axis=1, tiled=True)]
    dot_general x20 -> x0, matrix products: 76.5 us -> none  [the longest x2 14 us: spectra(): jnp.einsum('kbr,bd->krd', real_recv, -sine_q - cosine_q, precision=exact_...]
    all_to_all x11 -> x0, starting transfers between devices: 46.4 us -> none  [the longest x2 8.96 us: spectra(): lax.all_to_all(real_twist, 'seq', split_axis=2, concat_axis=1, tiled=True)]
    pallas_call x0 -> x1, Pallas kernels: none -> 40.5 us  [both_convs(): pl.pallas_call(functools.partial(conv_kernel, lags), grid=(count,), in_sp...]
    unnamed x24 -> x12, local copies, waits for them, and re-layouts: 5.27 us -> 0.71 us
    all_to_all x3 -> x2, blocking collectives: 38.1 us -> 34.9 us  [the longest x1 23.2 us: per_device(): got = lax.all_to_all(sent, 'seq', split_axis=0, concat_axis=0, tiled=True)]
  transfers between devices with their start and end apart: 11 -> 0, of which waited for: 11 -> 0; matrix products, arithmetic and copies ran while one was open for 2% -> 0% of each run, Pallas kernels for 0% -> 0%
where the time goes in v1:
time: 85.3 us; the launch traced here: 85 us
  Pallas kernels  40.5 us (47%)
  blocking collectives  36.9 us (43%)
  local copies, waits for them, and re-layouts  5.85 us (7%)
  other arithmetic  1.34 us (2%)
    pallas_call x1, Pallas kernels, both_convs(): pl.pallas_call(functools.partial(conv_kernel, lags), grid=(count,), in_sp...  40.5 us
    all_to_all x1, blocking collectives, per_device(): got = lax.all_to_all(sent, 'seq', split_axis=0, concat_axis=0, tiled=True)  23.2 us
    all_to_all x1, blocking collectives, per_device(): back = lax.all_to_all(back, 'seq', split_axis=0, concat_axis=0, tiled=True)  11.7 us
    all_gather x1, blocking collectives, per_device(): lax.all_gather(mixed_in, 'chan', axis=0, tiled=True)  1.99 us

profile of v1, /device:TPU:0, one launch (start us, length us, event | category | flops | bytes accessed | tf_op | source)
XLA Modules:
  0.0 85.0 jit_solution(17123706606024618222)
XLA Ops:
  0.0 0.0 copy-start
  0.0 0.7 copy-done.4
  0.7 0.0 copy-done.5
  0.7 1.2 %fusion.1 = (bf16[16,1,8,512]{3,2,1,0:T(8,128)(2,1)S(1)}, bf16[16,1,8,512]{3,2,1,0:T(8,128)(2,1)S(1)}) fusion(f32[128,512]{1,0:T(8,128)} %param.11, f32[128]{0:T(128)S(1)} %copy-done.4, pred[512]{0:T(512)(128)(4,1)S(1)} %fusion.3, f32[128,512]{1,0:T(8,128)} %param.12, f32[128]{0:T(128)S(1)} %copy-done.5), kind=kLoop, calls=%fused_computation.7 | loop fusion | flops 393216 | bytes 787968 | tf_op jit(solution)/shard_map/stack;reshape | solution.py:73
  1.9 0.0 copy-done.2
  1.9 0.0 copy-done.3
  1.9 0.1 pad_maximum_fusion
  2.0 23.2 %all_to_all.10 = bf16[16,4,8,512]{3,2,1,0:T(8,128)(2,1)S(1)} all-to-all(bf16[16,4,8,512]{3,2,1,0:T(8,128)(2,1)S(1)} %pad_maximum_fusion), channel_id=1, replica_groups=mesh['seq'=16,'chan'=2] {'seq'}, dimensions={0} | all-to-all | bytes 1048576 | tf_op jit(solution)/shard_map/all_to_all | solution.py:82
  25.2 0.1 slice_convert_fusion
  25.3 0.2 copy.18
  25.4 0.7 reshape.28.two
  26.2 0.7 squeeze.9.gate
  27.0 0.7 squeeze.8.values
  27.7 0.2 copy.17
  27.9 0.7 reshape.27.one
  28.6 40.5 %shard_map.82 = bf16[8,64,128]{2,1,0:T(8,128)(2,1)} custom-call(bf16[8,64,128]{2,1,0:T(8,128)(2,1)} %squeeze.8.values, bf16[8,64,128]{2,1,0:T(8,128)(2,1)} %squeeze.9.gate, f32[8,64,128]{2,1,0:T(8,128)} %reshape.27.one, f32[8,64,128]{2,1,0:T(8,128)} %reshape.28.two), custom_call_target="tpu_custom_call" | custom-call | tf_op jit(solution)/shard_map/pallas_call | solution.py:51
  69.1 1.0 %reshape.26 = bf16[8,16,512]{2,1,0:T(8,128)(2,1)S(1)} reshape(bf16[8,64,128]{2,1,0:T(8,128)(2,1)} %shard_map.82) | data formatting | bytes 262144 | tf_op jit(solution)/shard_map/reshape | solution.py:87
  70.1 0.1 copy.22
  70.2 0.0 copy-start.1
  70.2 11.7 %all_to_all.11 = bf16[16,8,512]{2,1,0:T(8,128)(2,1)S(1)} all-to-all(bf16[16,8,512]{2,1,0:T(8,128)(2,1)S(1)} %bitcast.28), channel_id=1, replica_groups=mesh['seq'=16,'chan'=2] {'seq'}, dimensions={0} | all-to-all | bytes 262144 | tf_op jit(solution)/shard_map/all_to_all | solution.py:88
  81.9 0.0 copy-done.1
  81.9 2.0 %all_gather.3 = bf16[256,512]{1,0:T(8,128)(2,1)S(1)} all-gather(bf16[128,512]{1,0:T(8,128)(2,1)S(1)} %fusion), channel_id=1, replica_groups=mesh['seq'=16,'chan'=2] {'chan'}, dimensions={0}, use_global_device_ids=true | all-gather | bytes 393216 | tf_op jit(solution)/shard_map/all_gather | solution.py:94
  83.9 0.3 multiply_convert_fusion
  84.2 0.8 copy.20
  (9 shorter events, 0.1 us)
Async XLA Ops:
  0.0 83.9 %copy-start = (bf16[256,128]{1,0:T(8,128)(2,1)S(1)}, bf16[256,128]{1,0:T(8,128)(2,1)}, u32[]{:S(2)}) copy-start(bf16[256,128]{1,0:T(8,128)(2,1)} %param.15) | copy-start | bytes 196612
  0.0 0.7 copy-start.4
  0.0 0.7 copy-start.5
  0.7 1.2 %copy-start.2 = (bf16[128,512]{1,0:T(8,128)(2,1)S(1)}, bf16[128,512]{1,0:T(8,128)(2,1)}, u32[]{:S(2)}) copy-start(bf16[128,512]{1,0:T(8,128)(2,1)} %param.9) | copy-start | bytes 393220
  0.7 1.2 %copy-start.3 = (bf16[128,512]{1,0:T(8,128)(2,1)S(1)}, bf16[128,512]{1,0:T(8,128)(2,1)}, u32[]{:S(2)}) copy-start(bf16[128,512]{1,0:T(8,128)(2,1)} %param.8) | copy-start | bytes 393220
  70.2 11.7 %copy-start.1 = (bf16[128,512]{1,0:T(8,128)(2,1)S(1)}, bf16[128,512]{1,0:T(8,128)(2,1)}, u32[]{:S(2)}) copy-start(bf16[128,512]{1,0:T(8,128)(2,1)} %param.10) | copy-start | bytes 393220

commit v2 on v1

v2 whole, which is shorter than its diff:
```python
import functools
import math

import jax
import jax.numpy as jnp
from jax import lax
from jax.experimental import pallas as pl
from jax.experimental.pallas import tpu as pltpu
from jax.sharding import PartitionSpec as P

LANES = 128
GROUP = 64


def toeplitz_conv(padded, taps, lags, exact):
    group_size = math.gcd(lags, GROUP)
    row = lax.broadcasted_iota(jnp.int32, (LANES, LANES), 0)
    lane = lax.broadcasted_iota(jnp.int32, (LANES, LANES), 1)
    lower = lane >= row

    def step(group, carry):
        total, before = carry
        left, rest, right = [], [], []
        for inner in range(group_size):
            lag = group * group_size + inner
            line = jnp.broadcast_to(taps[pl.ds(lag, 1), :], (LANES, LANES))
            turned = pltpu.roll(line, 0, 1, stride=1, stride_axis=0)
            right.append(jnp.where(lower, turned, before).astype(jnp.bfloat16))
            before = turned
            moved = padded[pl.ds(lags - lag, lags), :]
            left.append(moved.astype(jnp.bfloat16))
            if not exact:
                rest.append((moved - left[-1].astype(jnp.float32)).astype(jnp.bfloat16))
        rows = [jnp.concatenate(left, axis=1)]
        if not exact:
            rows.append(jnp.concatenate(rest, axis=1))
        sums = jnp.dot(
            jnp.concatenate(rows, axis=0),
            jnp.concatenate(right, axis=0),
            preferred_element_type=jnp.float32,
        )
        total = total + sums[:lags]
        if not exact:
            total = total + sums[lags:]
        return total, before

    start = (jnp.zeros((lags, LANES), jnp.float32), jnp.zeros((LANES, LANES), jnp.float32))
    if group_size == lags:
        return step(0, start)[0]
    return lax.fori_loop(0, lags // group_size, step, start)[0]


def conv_kernel(lags, values, gate, gate_out, one, two, out, padded):
    padded[pl.ds(0, lags), :] = jnp.zeros((lags, LANES), jnp.float32)
    padded[pl.ds(lags, lags), :] = values[0].astype(jnp.float32)
    first = toeplitz_conv(padded, one.at[0], lags, True)
    padded[pl.ds(lags, lags), :] = gate[0].astype(jnp.float32) * first
    second = toeplitz_conv(padded, two.at[0], lags, True)
    out[0] = (gate_out[0].astype(jnp.float32) * second).astype(out.dtype)


def both_convs(values, gate, gate_out, one, two):
    count, lags, _ = values.shape
    block = pl.BlockSpec((1, lags, LANES), lambda c: (c, 0, 0))
    return pl.pallas_call(
        functools.partial(conv_kernel, lags),
        grid=(count,),
        in_specs=[block] * 5,
        out_specs=block,
        out_shape=jax.ShapeDtypeStruct(values.shape, jnp.bfloat16),
        scratch_shapes=[pltpu.VMEM((2 * lags, LANES), jnp.float32)],
    )(values, gate, gate_out, one, two)


def per_device(seq, values, gate_one, gate_two, filter_one, filter_two, skip_one, skip_two, mix_weight):
    channels, tokens = values.shape
    each = -(-channels // seq)
    first_tap = (lax.iota(jnp.int32, tokens) == 0) & (lax.axis_index("seq") == 0)

    def with_skip(taps, skip):
        return (taps + jnp.where(first_tap[None, :], skip[:, None], 0.0)).astype(jnp.bfloat16)

    def spread(source):
        padded = jnp.pad(source, ((0, each * seq - channels), (0, 0)))
        return padded.reshape(seq, each, tokens)

    sent = jnp.stack(
        [
            spread(values),
            spread(gate_one),
            spread(gate_two),
            spread(with_skip(filter_one, skip_one)),
            spread(with_skip(filter_two, skip_two)),
        ],
        axis=1,
    )
    got = lax.all_to_all(sent, "seq", split_axis=0, concat_axis=0, tiled=True)
    lines = jnp.transpose(got, (1, 2, 0, 3)).reshape(5, each, seq * tokens // LANES, LANES)
    conv = both_convs(
        lines[0], lines[1], lines[2], lines[3].astype(jnp.float32), lines[4].astype(jnp.float32)
    )
    back = jnp.transpose(conv.reshape(each, seq, tokens), (1, 0, 2))
    back = lax.all_to_all(back, "seq", split_axis=0, concat_axis=0, tiled=True)
    mixed_in = back.reshape(each * seq, tokens)[:channels]
    summed = jnp.einsum(
        "de,dt->et",
        mix_weight,
        lax.all_gather(mixed_in, "chan", axis=0, tiled=True),
        preferred_element_type=jnp.float32,
    )
    return jax.nn.silu(summed).astype(jnp.bfloat16)


def solution(mesh):
    both = P("chan", "seq")
    return jax.shard_map(
        functools.partial(per_device, mesh.shape["seq"]),
        mesh=mesh,
        in_specs=(both, both, both, both, both, P("chan"), P("chan"), P(None, "chan")),
        out_specs=both,
        check_vma=False,
    )
```

time: 85.3 us -> 62.5 us (0.73)
  Pallas kernels: 40.5 us -> 13.2 us
  local copies, waits for them, and re-layouts: 5.85 us -> 8.71 us
  blocking collectives: 36.9 us -> 39.6 us
  other arithmetic: 1.34 us -> 0.24 us
    pallas_call x1, Pallas kernels: 40.5 us -> 13.2 us  [both_convs(): pl.pallas_call(functools.partial(conv_kernel, lags), grid=(count,), in_sp...]
    all_to_all x1, blocking collectives: 23.2 us -> 26.9 us  [per_device(): got = lax.all_to_all(sent, 'seq', split_axis=0, concat_axis=0, tiled=True)]
    unnamed x12 -> x17, local copies, waits for them, and re-layouts: 0.71 us -> 2.79 us
    another operation x2 -> x1, other arithmetic: 1.25 us -> 0.09 us  [per_device(): jnp.stack([spread(values), spread(gate_one), spread(gate_two), spread(wit...]
    all_to_all x1, blocking collectives: 11.7 us -> 10.7 us  [per_device(): back = lax.all_to_all(back, 'seq', split_axis=0, concat_axis=0, tiled=True)]
where the time goes in v2:
time: 62.5 us; the launch traced here: 62.1 us
  blocking collectives  39.6 us (63%)
  Pallas kernels  13.2 us (21%)
  local copies, waits for them, and re-layouts  8.71 us (14%)
    all_to_all x1, blocking collectives, per_device(): got = lax.all_to_all(sent, 'seq', split_axis=0, concat_axis=0, tiled=True)  26.9 us
    pallas_call x1, Pallas kernels, both_convs(): pl.pallas_call(functools.partial(conv_kernel, lags), grid=(count,), in_sp...  13.2 us
    all_to_all x1, blocking collectives, per_device(): back = lax.all_to_all(back, 'seq', split_axis=0, concat_axis=0, tiled=True)  10.7 us
    unnamed x17, local copies, waits for them, and re-layouts  2.79 us
    all_gather x1, blocking collectives, per_device(): lax.all_gather(mixed_in, 'chan', axis=0, tiled=True)  1.98 us

profile of v2, /device:TPU:0, one launch (start us, length us, event | category | flops | bytes accessed | tf_op | source)
XLA Modules:
  0.0 62.1 jit_solution(5887038532540698798)
XLA Ops:
  0.0 0.0 copy-start.4
  0.0 1.0 %bitcast_dynamic-update-slice_fusion.2 = bf16[16,5,8,512]{3,2,1,0:T(8,128)(2,1)S(1)} fusion(bf16[128,512]{1,0:T(8,128)(2,1)} %param.8), kind=kLoop, calls=%fused_computation.12 | loop fusion | bytes 262144
  1.0 0.0 copy-done.3
  1.0 0.0 copy-done.4
  1.1 0.9 %copy-done.1 = f32[128,512]{1,0:T(8,128)S(1)} copy-done((f32[128,512]{1,0:T(8,128)S(1)}, f32[128,512]{1,0:T(8,128)}, u32[]{:S(2)}) %copy-start.1) | copy-done | bytes 262168
  2.0 0.1 fusion.1
  2.1 0.9 %copy-done.2 = f32[128,512]{1,0:T(8,128)S(1)} copy-done((f32[128,512]{1,0:T(8,128)S(1)}, f32[128,512]{1,0:T(8,128)}, u32[]{:S(2)}) %copy-start.2) | copy-done | bytes 262168
  2.9 0.1 fusion.3
  3.0 26.9 %all_to_all.10 = bf16[16,5,8,512]{3,2,1,0:T(8,128)(2,1)S(1)} all-to-all(bf16[16,5,8,512]{3,2,1,0:T(8,128)(2,1)S(1)} %fusion.3), channel_id=1, replica_groups=mesh['seq'=16,'chan'=2] {'seq'}, dimensions={0} | all-to-all | bytes 1310720 | tf_op jit(solution)/shard_map/all_to_all | solution.py:97
  29.9 0.1 slice_convert_fusion
  30.0 0.2 copy.26
  30.2 0.7 %reshape.31.two = f32[8,64,128]{2,1,0:T(8,128)} reshape(f32[1,8,16,512]{3,2,1,0:T(8,128)S(1)} %copy.26) | data formatting | bytes 524288 | tf_op jit(solution)/shard_map/convert_element_type | solution.py:100
  30.9 0.7 %squeeze.13.gate_out = bf16[8,64,128]{2,1,0:T(8,128)(2,1)} reshape(bf16[1,8,16,512]{3,2,1,0:T(8,128)(2,1)S(1)} %copy.24) | data formatting | bytes 262144 | tf_op jit(solution)/shard_map/squeeze | solution.py:100
  31.7 0.7 %squeeze.12.gate = bf16[8,64,128]{2,1,0:T(8,128)(2,1)} reshape(bf16[1,8,16,512]{3,2,1,0:T(8,128)(2,1)S(1)} %copy.23) | data formatting | bytes 262144 | tf_op jit(solution)/shard_map/squeeze | solution.py:100
  32.5 0.7 %squeeze.11.values = bf16[8,64,128]{2,1,0:T(8,128)(2,1)} reshape(bf16[1,8,16,512]{3,2,1,0:T(8,128)(2,1)S(1)} %copy.22) | data formatting | bytes 262144 | tf_op jit(solution)/shard_map/squeeze | solution.py:100
  33.2 0.2 copy.25
  33.4 0.7 %reshape.30.one = f32[8,64,128]{2,1,0:T(8,128)} reshape(f32[1,8,16,512]{3,2,1,0:T(8,128)S(1)} %copy.25) | data formatting | bytes 524288 | tf_op jit(solution)/shard_map/convert_element_type | solution.py:100
  34.1 13.2 %shard_map.82 = bf16[8,64,128]{2,1,0:T(8,128)(2,1)} custom-call(bf16[8,64,128]{2,1,0:T(8,128)(2,1)} %squeeze.11.values, bf16[8,64,128]{2,1,0:T(8,128)(2,1)} %squeeze.12.gate, bf16[8,64,128]{2,1,0:T(8,128)(2,1)} %squeeze.13.gate_out, f32[8,64,128]{2,1,0:T(8,128)} %reshape.30.one, f32[8,64,128]{2,1,0:T(8,128)} %reshape.31.two), custom_call_target="tpu_custom_call" | custom-call | tf_op jit(solution)/shard_map/pallas_call | solution.py:65
  47.3 1.0 %reshape.28 = bf16[8,16,512]{2,1,0:T(8,128)(2,1)S(1)} reshape(bf16[8,64,128]{2,1,0:T(8,128)(2,1)} %shard_map.82) | data formatting | bytes 262144 | tf_op jit(solution)/shard_map/reshape | solution.py:102
  48.3 0.1 copy.30
  48.4 10.7 %all_to_all.11 = bf16[16,8,512]{2,1,0:T(8,128)(2,1)S(1)} all-to-all(bf16[16,8,512]{2,1,0:T(8,128)(2,1)S(1)} %bitcast.37), channel_id=1, replica_groups=mesh['seq'=16,'chan'=2] {'seq'}, dimensions={0} | all-to-all | bytes 262144 | tf_op jit(solution)/shard_map/all_to_all | solution.py:103
  59.1 2.0 %all_gather.3 = bf16[256,512]{1,0:T(8,128)(2,1)S(1)} all-gather(bf16[128,512]{1,0:T(8,128)(2,1)S(1)} %bitcast.36), channel_id=1, replica_groups=mesh['seq'=16,'chan'=2] {'chan'}, dimensions={0}, use_global_device_ids=true | all-gather | bytes 393216 | tf_op jit(solution)/shard_map/all_gather | solution.py:108
  61.1 0.3 multiply_convert_fusion
  61.3 0.8 %copy.28 = bf16[128,512]{1,0:T(8,128)(2,1)} copy(bf16[128,512]{0,1:T(8,128)(2,1)S(1)} %multiply_convert_fusion) | data formatting | bytes 262144 | tf_op jit(solution)/shard_map/convert_element_type | solution.py:111
  (15 shorter events, 0.2 us)
Async XLA Ops:
  0.0 61.1 %copy-start = (bf16[256,128]{1,0:T(8,128)(2,1)S(1)}, bf16[256,128]{1,0:T(8,128)(2,1)}, u32[]{:S(2)}) copy-start(bf16[256,128]{1,0:T(8,128)(2,1)} %param.15) | copy-start | bytes 196612
  0.0 1.0 %copy-start.3 = (bf16[128,512]{1,0:T(8,128)(2,1)S(1)}, bf16[128,512]{1,0:T(8,128)(2,1)}, u32[]{:S(2)}) copy-start(bf16[128,512]{1,0:T(8,128)(2,1)} %param.9) | copy-start | bytes 393220
  0.0 1.1 %copy-start.4 = (bf16[128,512]{1,0:T(8,128)(2,1)S(1)}, bf16[128,512]{1,0:T(8,128)(2,1)}, u32[]{:S(2)}) copy-start(bf16[128,512]{1,0:T(8,128)(2,1)} %param.10) | copy-start | bytes 393220
  1.0 1.0 %copy-start.1 = (f32[128,512]{1,0:T(8,128)S(1)}, f32[128,512]{1,0:T(8,128)}, u32[]{:S(2)}) copy-start(f32[128,512]{1,0:T(8,128)} %param.11) | copy-start | bytes 786436
  1.1 0.9 %copy-start.5 = (f32[128]{0:T(128)S(1)}, f32[128]{0:T(128)}, u32[]{:S(2)}) copy-start(f32[128]{0:T(128)} %param.13) | copy-start | bytes 1540
  2.0 1.0 %copy-start.2 = (f32[128,512]{1,0:T(8,128)S(1)}, f32[128,512]{1,0:T(8,128)}, u32[]{:S(2)}) copy-start(f32[128,512]{1,0:T(8,128)} %param.12) | copy-start | bytes 786436
  2.0 1.0 %copy-start.6 = (f32[128]{0:T(128)S(1)}, f32[128]{0:T(128)}, u32[]{:S(2)}) copy-start(f32[128]{0:T(128)} %param.14) | copy-start | bytes 1540

commit v3 on v1

v3 whole, which is shorter than its diff:
```python
import functools
import math

import jax
import jax.numpy as jnp
from jax import lax
from jax.experimental import pallas as pl
from jax.experimental.pallas import tpu as pltpu
from jax.sharding import PartitionSpec as P

LANES = 128
GROUP = 64
PARTS = 1
MESH = pl.DeviceIdType.MESH


def toeplitz_conv(padded, taps, lags):
    group_size = math.gcd(lags, GROUP)
    row = lax.broadcasted_iota(jnp.int32, (LANES, LANES), 0)
    lane = lax.broadcasted_iota(jnp.int32, (LANES, LANES), 1)
    lower = lane >= row

    def step(group, carry):
        total, before = carry
        left, right = [], []
        for inner in range(group_size):
            lag = group * group_size + inner
            line = jnp.broadcast_to(taps[pl.ds(lag, 1), :], (LANES, LANES))
            turned = pltpu.roll(line, 0, 1, stride=1, stride_axis=0)
            right.append(jnp.where(lower, turned, before).astype(jnp.bfloat16))
            before = turned
            left.append(padded[pl.ds(lags - lag, lags), :].astype(jnp.bfloat16))
        total = total + jnp.dot(
            jnp.concatenate(left, axis=1),
            jnp.concatenate(right, axis=0),
            preferred_element_type=jnp.float32,
        )
        return total, before

    start = (jnp.zeros((lags, LANES), jnp.float32), jnp.zeros((LANES, LANES), jnp.float32))
    if group_size == lags:
        return step(0, start)[0]
    return lax.fori_loop(0, lags // group_size, step, start)[0]


def rows_of(start, count, stride):
    return pl.ds(start, count, stride=stride) if count > 1 else pl.ds(start, 1)


def layer_kernel(
    seq, chan, each, parts, tokens,
    early, late, mix, out,
    got_early, got_late, lines, padded, ready, full, wide,
    early_out, early_in, late_out, late_in, back_out, back_in, pass_out, pass_in, own,
):
    me, mine = lax.axis_index("seq"), lax.axis_index("chan")
    tiles = tokens // LANES
    lags = seq * tiles
    share = each // parts

    def other(offset):
        return lax.rem(me + offset, seq)

    def sibling(offset):
        return lax.rem(mine + offset, chan)

    def to_peer(source, target, sent, landed, peer):
        return pltpu.make_async_remote_copy(
            src_ref=source, dst_ref=target, send_sem=sent, recv_sem=landed,
            device_id=(peer, mine), device_id_type=MESH,
        )

    def early_copy(peer, slot):
        return to_peer(early.at[peer], got_early.at[slot], early_out.at[peer], early_in.at[slot], peer)

    def late_copy(peer, slot):
        return to_peer(late.at[peer], got_late.at[slot], late_out.at[peer], late_in.at[slot], peer)

    def back_copy(part, peer, slot):
        return to_peer(
            ready.at[part, peer], full.at[mine, slot, part],
            back_out.at[part, peer], back_in.at[part, slot], peer,
        )

    def pass_copy(part, slot, group, offset):
        return pltpu.make_async_remote_copy(
            src_ref=full.at[group, slot, part], dst_ref=full.at[group, slot, part],
            send_sem=pass_out.at[part, offset, slot], recv_sem=pass_in.at[part, group, slot],
            device_id=(me, sibling(offset)), device_id_type=MESH,
        )

    def each_other(body):
        def step(offset, carry):
            body(other(offset))
            return carry

        lax.fori_loop(1, seq, step, 0)

    barrier = pltpu.get_barrier_semaphore()
    each_other(
        lambda peer: pl.semaphore_signal(barrier, inc=1, device_id=(peer, mine), device_id_type=MESH)
    )
    for offset in range(1, chan):
        pl.semaphore_signal(barrier, inc=1, device_id=(me, sibling(offset)), device_id_type=MESH)
    pl.semaphore_wait(barrier, seq - 1 + chan - 1)

    each_other(lambda peer: early_copy(peer, me).start())
    each_other(lambda peer: late_copy(peer, me).start())
    own_early = pltpu.make_async_copy(early.at[me], got_early.at[me], own.at[0])
    own_late = pltpu.make_async_copy(late.at[me], got_late.at[me], own.at[1])
    own_early.start()
    own_late.start()
    padded[pl.ds(0, lags), :] = jnp.zeros((lags, LANES), jnp.float32)

    def lay_out(got, piece, first):
        def step(source, carry):
            for index in range(got.shape[1]):
                block = got[source, index].astype(jnp.float32)
                for tile in range(tiles):
                    lines[first + index, rows_of(source * tiles + tile, each, lags), :] = block[
                        :, tile * LANES : (tile + 1) * LANES
                    ]
            return carry

        lax.fori_loop(0, seq, step, 0)

    each_other(lambda peer: early_copy(peer, peer).wait_recv())
    own_early.wait()
    lay_out(got_early, 2, 0)

    def first_conv(channel, carry):
        base = pl.multiple_of(channel * lags, lags)
        padded[pl.ds(lags, lags), :] = lines[0, pl.ds(base, lags), :]
        lines[0, pl.ds(base, lags), :] = toeplitz_conv(padded, lines.at[1, pl.ds(base, lags)], lags)
        return carry

    lax.fori_loop(0, each, first_conv, 0)

    each_other(lambda peer: late_copy(peer, peer).wait_recv())
    own_late.wait()
    lay_out(got_late, 3, 2)

    def second_conv(channel, carry):
        base = pl.multiple_of(channel * lags, lags)
        here = pl.ds(base, lags)
        padded[pl.ds(lags, lags), :] = lines[2, here, :] * lines[0, here, :]
        second = toeplitz_conv(padded, lines.at[4, here], lags)
        lines[0, here, :] = lines[3, here, :] * second
        return carry

    own_back = []
    for part in range(parts):
        lax.fori_loop(part * share, (part + 1) * share, second_conv, 0)

        def gather(target, carry, part=part):
            for tile in range(tiles):
                ready[part, target, :, pl.ds(tile * LANES, LANES)] = lines[
                    0, rows_of(part * share * lags + target * tiles + tile, share, lags), :
                ].astype(ready.dtype)
            return carry

        lax.fori_loop(0, seq, gather, 0)
        each_other(lambda peer, part=part: back_copy(part, peer, me).start())
        own_back.append(
            pltpu.make_async_copy(ready.at[part, me], full.at[mine, me, part], own.at[2 + part])
        )
        own_back[-1].start()

    def pass_on(part, slot):
        for offset in range(1, chan):
            pass_copy(part, slot, mine, offset).start()

    for part in range(parts):
        own_back[part].wait()
        pass_on(part, me)

        def arrived(peer, part=part):
            back_copy(part, peer, peer).wait_recv()
            pass_on(part, peer)

        each_other(arrived)

    def widen(group, slot):
        for part in range(parts):
            wide[pl.ds((group * seq + slot) * each + part * share, share), :] = full[
                group, slot, part
            ].astype(jnp.float32)

    def widen_mine(slot, carry):
        widen(mine, slot)
        return carry

    lax.fori_loop(0, seq, widen_mine, 0)
    for offset in range(1, chan):
        group = sibling(offset)

        def widen_other(slot, carry, group=group, offset=offset):
            for part in range(parts):
                pass_copy(part, slot, group, offset).wait_recv()
            widen(group, slot)
            return carry

        lax.fori_loop(0, seq, widen_other, 0)

    summed = jnp.dot(mix[...], wide[...].astype(jnp.bfloat16), preferred_element_type=jnp.float32)
    out[...] = (summed / (1.0 + jnp.exp(-summed))).astype(out.dtype)

    each_other(lambda peer: early_copy(peer, me).wait_send())
    each_other(lambda peer: late_copy(peer, me).wait_send())
    for part in range(parts):
        each_other(lambda peer, part=part: back_copy(part, peer, me).wait_send())
        for offset in range(1, chan):

            def sent(slot, carry, part=part, offset=offset):
                pass_copy(part, slot, mine, offset).wait_send()
                return carry

            lax.fori_loop(0, seq, sent, 0)


def per_device(
    seq, chan, values, gate_one, gate_two, filter_one, filter_two, skip_one, skip_two, mix_weight
):
    channels, tokens = values.shape
    made = mix_weight.shape[1]
    each = -(-channels // seq)
    parts = math.gcd(each, PARTS)
    lags = seq * tokens // LANES
    room = each * seq
    first_tap = (lax.iota(jnp.int32, tokens) == 0) & (lax.axis_index("seq") == 0)

    def with_skip(taps, skip):
        return (taps + jnp.where(first_tap[None, :], skip[:, None], 0.0)).astype(jnp.bfloat16)

    def spread(*sources):
        return jnp.stack(
            [
                jnp.pad(source, ((0, room - channels), (0, 0))).reshape(seq, each, tokens)
                for source in sources
            ],
            axis=1,
        )

    early = spread(values, with_skip(filter_one, skip_one))
    late = spread(gate_one, gate_two, with_skip(filter_two, skip_two))
    mix = jnp.pad(
        mix_weight.T.reshape(made, chan, channels), ((0, 0), (0, 0), (0, room - channels))
    ).reshape(made, chan * room)
    anywhere = pl.BlockSpec(memory_space=pl.ANY)
    vmem = pl.BlockSpec(memory_space=pltpu.VMEM)
    dma = pltpu.SemaphoreType.DMA
    share = each // parts
    return pl.pallas_call(
        functools.partial(layer_kernel, seq, chan, each, parts, tokens),
        in_specs=[anywhere, anywhere, vmem],
        out_specs=vmem,
        out_shape=jax.ShapeDtypeStruct((made, tokens), jnp.bfloat16),
        scratch_shapes=[
            pltpu.VMEM((seq, 2, each, tokens), jnp.bfloat16),
            pltpu.VMEM((seq, 3, each, tokens), jnp.bfloat16),
            pltpu.VMEM((5, each * lags, LANES), jnp.float32),
            pltpu.VMEM((2 * lags, LANES), jnp.float32),
            pltpu.VMEM((parts, seq, share, tokens), jnp.bfloat16),
            pltpu.VMEM((chan, seq, parts, share, tokens), jnp.bfloat16),
            pltpu.VMEM((chan * room, tokens), jnp.float32),
            dma((seq,)),
            dma((seq,)),
            dma((seq,)),
            dma((seq,)),
            dma((parts, seq)),
            dma((parts, seq)),
            dma((parts, chan, seq)),
            dma((parts, chan, seq)),
            dma((2 + parts,)),
        ],
        compiler_params=pltpu.CompilerParams(collective_id=0, has_side_effects=True),
    )(early, late, mix)


def solution(mesh):
    both = P("chan", "seq")
    return jax.shard_map(
        functools.partial(per_device, mesh.shape["seq"], mesh.shape["chan"]),
        mesh=mesh,
        in_specs=(both, both, both, both, both, P("chan"), P("chan"), P(None, "chan")),
        out_specs=both,
        check_vma=False,
    )
```

time: 85.3 us -> 47.8 us (0.56)
  blocking collectives: 36.9 us -> 0 us
  local copies, waits for them, and re-layouts: 5.85 us -> 3.93 us
  other arithmetic: 1.34 us -> 2.7 us
    all_to_all x2 -> x0, blocking collectives: 34.9 us -> none  [the longest x1 23.2 us: per_device(): got = lax.all_to_all(sent, 'seq', split_axis=0, concat_axis=0, tiled=True)]
    unnamed x12, local copies, waits for them, and re-layouts: 0.71 us -> 3.93 us
    convert_element_type x5 -> x0, local copies, waits for them, and re-layouts: 2.52 us -> none  [the longest x2 0.87 us: per_device(): lines[3].astype(jnp.float32)]
    all_gather x1 -> x0, blocking collectives: 1.99 us -> none  [per_device(): lax.all_gather(mixed_in, 'chan', axis=0, tiled=True)]
    squeeze x2 -> x0, local copies, waits for them, and re-layouts: 1.47 us -> none  [the longest x1 0.74 us: per_device(): lines[0]]
    another operation x2 -> x3, other arithmetic: 1.25 us -> 2.69 us  [spread(): jnp.stack([jnp.pad(source, ((0, room - channels), (0, 0))).reshape(seq, e...]
    reshape x2 -> x0, local copies, waits for them, and re-layouts: 1.07 us -> none  [per_device(): back = jnp.transpose(conv.reshape(each, seq, tokens), (1, 0, 2))]
where the time goes in v3:
time: 47.8 us; the launch traced here: 47 us
  Pallas kernels  40.3 us (84%)
  local copies, waits for them, and re-layouts  3.93 us (8%)
  other arithmetic  2.7 us (6%)
    pallas_call x1, Pallas kernels, per_device(): pl.pallas_call(functools.partial(layer_kernel, seq, chan, each, parts, to...  40.3 us
    unnamed x12, local copies, waits for them, and re-layouts  3.93 us
    another operation x3, other arithmetic, spread(): jnp.stack([jnp.pad(source, ((0, room - channels), (0, 0))).reshape(seq, e...  2.69 us

profile of v3, /device:TPU:0, one launch (start us, length us, event | category | flops | bytes accessed | tf_op | source)
XLA Modules:
  0.0 47.0 jit_solution(11439580254270419057)
XLA Ops:
  0.0 1.6 %copy.9 = bf16[256,128]{0,1:T(8,128)(2,1)} copy(bf16[256,128]{1,0:T(8,128)(2,1)} %param.15) | data formatting | bytes 131072 | tf_op args[7]
  1.6 0.0 copy-start.3
  1.6 0.0 copy-start.4
  1.6 0.7 %copy-done.3 = f32[128]{0:T(128)S(1)} copy-done((f32[128]{0:T(128)S(1)}, f32[128]{0:T(128)}, u32[]{:S(2)}) %copy-start.3) | copy-done | bytes 536
  2.2 0.0 copy-done.4
  2.3 0.0 copy-start
  2.3 0.0 copy-start.1
  2.3 1.2 %fusion.1 = (bf16[16,1,8,512]{3,2,1,0:T(8,128)(2,1)S(1)}, bf16[16,1,8,512]{3,2,1,0:T(8,128)(2,1)S(1)}) fusion(f32[128,512]{1,0:T(8,128)} %param.12, f32[128]{0:T(128)S(1)} %copy-done.3, pred[512]{0:T(512)(128)(4,1)S(1)} %fusion.2, f32[128,512]{1,0:T(8,128)} %param.11, f32[128]{0:T(128)S(1)} %copy-done.4), kind=kLoop, calls=%fused_computation.5 | loop fusion | flops 393216 | bytes 787968 | tf_op jit(solution)/shard_map/stack;reshape | solution.py:236
  3.4 0.0 copy-done
  3.5 0.0 copy-done.1
  3.5 0.0 copy-start.2
  3.5 0.8 %pad_maximum_fusion.late = bf16[16,3,8,512]{3,2,1,0:T(8,128)(2,1)} fusion(bf16[16,1,8,512]{3,2,1,0:T(8,128)(2,1)S(1)} %get-tuple-element.5, bf16[16,1,8,512]{3,2,1,0:T(8,128)(2,1)S(1)} %bitcast.9, bf16[16,1,8,512]{3,2,1,0:T(8,128)(2,1)S(1)} %bitcast.10), kind=kLoop, calls=%fused_computation | loop fusion | flops 393216 | bytes 786432 | tf_op jit(solution)/shard_map/stack | solution.py:236
  4.3 0.1 copy-done.2
  4.4 0.7 %pad_maximum_fusion.1.early = bf16[16,2,8,512]{3,2,1,0:T(8,128)(2,1)} fusion(bf16[16,1,8,512]{3,2,1,0:T(8,128)(2,1)S(1)} %get-tuple-element.6, bf16[16,1,8,512]{3,2,1,0:T(8,128)(2,1)S(1)} %bitcast.11), kind=kLoop, calls=%fused_computation.1 | loop fusion | flops 131072 | bytes 524288 | tf_op jit(solution)/shard_map/stack | solution.py:236
  5.1 40.3 %shard_map.82 = bf16[128,512]{1,0:T(8,128)(2,1)} custom-call(bf16[16,2,8,512]{3,2,1,0:T(8,128)(2,1)} %pad_maximum_fusion.1.early, bf16[16,3,8,512]{3,2,1,0:T(8,128)(2,1)} %pad_maximum_fusion.late, bf16[128,256]{1,0:T(8,128)(2,1)} %bitcast.8), custom_call_target="tpu_custom_call" | custom-call | tf_op jit(solution)/shard_map/pallas_call | solution.py:253
  45.4 1.6 %copy.11 = bf16[128,512]{1,0:T(8,128)(2,1)} copy(bf16[128,512]{1,0:T(8,128)(2,1)} %shard_map.82) | data formatting | bytes 262144
  (1 shorter events, 0.0 us)
Async XLA Ops:
  1.6 0.7 %copy-start.3 = (f32[128]{0:T(128)S(1)}, f32[128]{0:T(128)}, u32[]{:S(2)}) copy-start(f32[128]{0:T(128)} %param.14) | copy-start | bytes 1540
  1.6 0.7 %copy-start.4 = (f32[128]{0:T(128)S(1)}, f32[128]{0:T(128)}, u32[]{:S(2)}) copy-start(f32[128]{0:T(128)} %param.13) | copy-start | bytes 1540
  2.3 1.2 %copy-start = (bf16[128,512]{1,0:T(8,128)(2,1)S(1)}, bf16[128,512]{1,0:T(8,128)(2,1)}, u32[]{:S(2)}) copy-start(bf16[128,512]{1,0:T(8,128)(2,1)} %param.10) | copy-start | bytes 393220
  2.3 1.2 %copy-start.1 = (bf16[128,512]{1,0:T(8,128)(2,1)S(1)}, bf16[128,512]{1,0:T(8,128)(2,1)}, u32[]{:S(2)}) copy-start(bf16[128,512]{1,0:T(8,128)(2,1)} %param.9) | copy-start | bytes 393220
  3.5 0.9 %copy-start.2 = (bf16[128,512]{1,0:T(8,128)(2,1)S(1)}, bf16[128,512]{1,0:T(8,128)(2,1)}, u32[]{:S(2)}) copy-start(bf16[128,512]{1,0:T(8,128)(2,1)} %param.8) | copy-start | bytes 393220

commit v4 on v3

--- a/solution.py
+++ b/solution.py
@@ -49,9 +49,9 @@
 
 def layer_kernel(
     seq, chan, each, parts, tokens,
-    early, late, mix, out,
-    got_early, got_late, lines, padded, ready, full, wide,
-    early_out, early_in, late_out, late_in, back_out, back_in, pass_out, pass_in, own,
+    values, gate_one, gate_two, filter_one, filter_two, skip_one, skip_two, mix, out,
+    taps_one, taps_two, direct, got, lines, padded, ready, full, wide,
+    sent_out, sent_in, back_out, back_in, pass_out, pass_in, own,
 ):
     me, mine = lax.axis_index("seq"), lax.axis_index("chan")
     tiles = tokens // LANES
@@ -70,11 +70,14 @@
             device_id=(peer, mine), device_id_type=MESH,
         )
 
-    def early_copy(peer, slot):
-        return to_peer(early.at[peer], got_early.at[slot], early_out.at[peer], early_in.at[slot], peer)
-
-    def late_copy(peer, slot):
-        return to_peer(late.at[peer], got_late.at[slot], late_out.at[peer], late_in.at[slot], peer)
+    pieces = (values, taps_one, gate_one, taps_two, gate_two)
+    early, late = (0, 1), (2, 3, 4)
+
+    def piece_copy(piece, peer, slot):
+        return to_peer(
+            pieces[piece].at[peer], got.at[piece, slot],
+            sent_out.at[piece, peer], sent_in.at[piece, slot], peer,
+        )
 
     def back_copy(part, peer, slot):
         return to_peer(
@@ -102,31 +105,63 @@
     )
     for offset in range(1, chan):
         pl.semaphore_signal(barrier, inc=1, device_id=(me, sibling(offset)), device_id_type=MESH)
+    room = seq * each
+    for taps, source, skip in ((taps_one, filter_one, skip_one), (taps_two, filter_two, skip_two)):
+        row = lax.broadcasted_iota(jnp.int32, (room, room), 0)
+        lane = lax.broadcasted_iota(jnp.int32, (room, room), 1)
+        column = jnp.sum(
+            jnp.where(row == lane, jnp.broadcast_to(skip[...], (room, room)), 0.0), axis=1, keepdims=True
+        )
+        lane = lax.broadcasted_iota(jnp.int32, (room, LANES), 1)
+        direct[...] = jnp.where(lane + me == 0, column, 0.0)
+
+        def make_taps(target, carry, taps=taps, source=source):
+            for tile in range(tiles):
+                part = source[target, :, pl.ds(tile * LANES, LANES)]
+                if tile == 0:
+                    part = part + direct[pl.ds(target * each, each), :]
+                taps[target, :, pl.ds(tile * LANES, LANES)] = part.astype(taps.dtype)
+            return carry
+
+        lax.fori_loop(0, seq, make_taps, 0)
     pl.semaphore_wait(barrier, seq - 1 + chan - 1)
 
-    each_other(lambda peer: early_copy(peer, me).start())
-    each_other(lambda peer: late_copy(peer, me).start())
-    own_early = pltpu.make_async_copy(early.at[me], got_early.at[me], own.at[0])
-    own_late = pltpu.make_async_copy(late.at[me], got_late.at[me], own.at[1])
-    own_early.start()
-    own_late.start()
+    own_copies = [
+        pltpu.make_async_copy(pieces[piece].at[me], got.at[piece, me], own.at[piece])
+        for piece in early + late
+    ]
+    for group in (early, late):
+
+        def send(peer, group=group):
+            for piece in group:
+                piece_copy(piece, peer, me).start()
+
+        each_other(send)
+        for piece in group:
+            own_copies[piece].start()
     padded[pl.ds(0, lags), :] = jnp.zeros((lags, LANES), jnp.float32)
 
-    def lay_out(got, piece, first):
+    def lay_out(group):
+        def wait(peer):
+            for piece in group:
+                piece_copy(piece, peer, peer).wait_recv()
+
+        each_other(wait)
+        for piece in group:
+            own_copies[piece].wait()
+
         def step(source, carry):
-            for index in range(got.shape[1]):
-                block = got[source, index].astype(jnp.float32)
+            for piece in group:
+                block = got[piece, source].astype(jnp.float32)
                 for tile in range(tiles):
-                    lines[first + index, rows_of(source * tiles + tile, each, lags), :] = block[
+                    lines[piece, rows_of(source * tiles + tile, each, lags), :] = block[
                         :, tile * LANES : (tile + 1) * LANES
                     ]
             return carry
 
         lax.fori_loop(0, seq, step, 0)
 
-    each_other(lambda peer: early_copy(peer, peer).wait_recv())
-    own_early.wait()
-    lay_out(got_early, 2, 0)
+    lay_out(early)
 
     def first_conv(channel, carry):
         base = pl.multiple_of(channel * lags, lags)
@@ -136,16 +171,14 @@
 
     lax.fori_loop(0, each, first_conv, 0)
 
-    each_other(lambda peer: late_copy(peer, peer).wait_recv())
-    own_late.wait()
-    lay_out(got_late, 3, 2)
+    lay_out(late)
 
     def second_conv(channel, carry):
         base = pl.multiple_of(channel * lags, lags)
         here = pl.ds(base, lags)
         padded[pl.ds(lags, lags), :] = lines[2, here, :] * lines[0, here, :]
-        second = toeplitz_conv(padded, lines.at[4, here], lags)
-        lines[0, here, :] = lines[3, here, :] * second
+        second = toeplitz_conv(padded, lines.at[3, here], lags)
+        lines[0, here, :] = lines[4, here, :] * second
         return carry
 
     own_back = []
@@ -162,7 +195,7 @@
         lax.fori_loop(0, seq, gather, 0)
         each_other(lambda peer, part=part: back_copy(part, peer, me).start())
         own_back.append(
-            pltpu.make_async_copy(ready.at[part, me], full.at[mine, me, part], own.at[2 + part])
+            pltpu.make_async_copy(ready.at[part, me], full.at[mine, me, part], own.at[len(pieces) + part])
         )
         own_back[-1].start()
 
@@ -202,11 +235,15 @@
 
         lax.fori_loop(0, seq, widen_other, 0)
 
-    summed = jnp.dot(mix[...], wide[...].astype(jnp.bfloat16), preferred_element_type=jnp.float32)
-    out[...] = (summed / (1.0 + jnp.exp(-summed))).astype(out.dtype)
-
-    each_other(lambda peer: early_copy(peer, me).wait_send())
-    each_other(lambda peer: late_copy(peer, me).wait_send())
+    out[...] = lax.dot_general(
+        mix[...],
+        wide[...].astype(jnp.bfloat16),
+        (((0,), (0,)), ((), ())),
+        preferred_element_type=jnp.float32,
+    )
+
+    for piece in early + late:
+        each_other(lambda peer, piece=piece: piece_copy(piece, peer, me).wait_send())
     for part in range(parts):
         each_other(lambda peer, part=part: back_copy(part, peer, me).wait_send())
         for offset in range(1, chan):
@@ -227,54 +264,49 @@
     parts = math.gcd(each, PARTS)
     lags = seq * tokens // LANES
     room = each * seq
-    first_tap = (lax.iota(jnp.int32, tokens) == 0) & (lax.axis_index("seq") == 0)
-
-    def with_skip(taps, skip):
-        return (taps + jnp.where(first_tap[None, :], skip[:, None], 0.0)).astype(jnp.bfloat16)
-
-    def spread(*sources):
-        return jnp.stack(
-            [
-                jnp.pad(source, ((0, room - channels), (0, 0))).reshape(seq, each, tokens)
-                for source in sources
-            ],
-            axis=1,
-        )
-
-    early = spread(values, with_skip(filter_one, skip_one))
-    late = spread(gate_one, gate_two, with_skip(filter_two, skip_two))
+
+    def spread(source):
+        return jnp.pad(source, ((0, room - channels), (0, 0))).reshape(seq, each, tokens)
+
+    def lane_row(skip):
+        return jnp.pad(skip, (0, room - channels)).reshape(1, room)
+
     mix = jnp.pad(
-        mix_weight.T.reshape(made, chan, channels), ((0, 0), (0, 0), (0, room - channels))
-    ).reshape(made, chan * room)
+        mix_weight.reshape(chan, channels, made), ((0, 0), (0, room - channels), (0, 0))
+    ).reshape(chan * room, made)
     anywhere = pl.BlockSpec(memory_space=pl.ANY)
     vmem = pl.BlockSpec(memory_space=pltpu.VMEM)
     dma = pltpu.SemaphoreType.DMA
     share = each // parts
-    return pl.pallas_call(
+    summed = pl.pallas_call(
         functools.partial(layer_kernel, seq, chan, each, parts, tokens),
-        in_specs=[anywhere, anywhere, vmem],
+        in_specs=[anywhere] * 3 + [vmem] * 5,
         out_specs=vmem,
-        out_shape=jax.ShapeDtypeStruct((made, tokens), jnp.bfloat16),
+        out_shape=jax.ShapeDtypeStruct((made, tokens), jnp.float32),
         scratch_shapes=[
-            pltpu.VMEM((seq, 2, each, tokens), jnp.bfloat16),
-            pltpu.VMEM((seq, 3, each, tokens), jnp.bfloat16),
+            pltpu.VMEM((seq, each, tokens), jnp.bfloat16),
+            pltpu.VMEM((seq, each, tokens), jnp.bfloat16),
+            pltpu.VMEM((room, LANES), jnp.float32),
+            pltpu.VMEM((5, seq, each, tokens), jnp.bfloat16),
             pltpu.VMEM((5, each * lags, LANES), jnp.float32),
             pltpu.VMEM((2 * lags, LANES), jnp.float32),
             pltpu.VMEM((parts, seq, share, tokens), jnp.bfloat16),
             pltpu.VMEM((chan, seq, parts, share, tokens), jnp.bfloat16),
             pltpu.VMEM((chan * room, tokens), jnp.float32),
-            dma((seq,)),
-            dma((seq,)),
-            dma((seq,)),
-            dma((seq,)),
+            dma((5, seq)),
+            dma((5, seq)),
             dma((parts, seq)),
             dma((parts, seq)),
             dma((parts, chan, seq)),
             dma((parts, chan, seq)),
-            dma((2 + parts,)),
+            dma((5 + parts,)),
         ],
         compiler_params=pltpu.CompilerParams(collective_id=0, has_side_effects=True),
-    )(early, late, mix)
+    )(
+        spread(values), spread(gate_one), spread(gate_two), spread(filter_one), spread(filter_two),
+        lane_row(skip_one), lane_row(skip_two), mix,
+    )
+    return (summed / (1.0 + jnp.exp(-summed))).astype(jnp.bfloat16)
 
 
 def solution(mesh):

time: 47.8 us -> 44.7 us (0.935)
  local copies, waits for them, and re-layouts: 3.93 us -> 0 us
  Pallas kernels: 40.3 us -> 42.5 us
  other arithmetic: 2.7 us -> 1.68 us
    unnamed x12 -> x0, local copies, waits for them, and re-layouts: 3.93 us -> none
    another operation x3 -> x0, other arithmetic: 2.69 us -> none  [spread(): jnp.stack([jnp.pad(source, ((0, room - channels), (0, 0))).reshape(seq, e...]
    pallas_call x1, Pallas kernels: 40.3 us -> 42.5 us  [per_device(): pl.pallas_call(functools.partial(layer_kernel, seq, chan, each, parts, to...]
    convert_element_type x0 -> x1, other arithmetic: none -> 1.68 us  [per_device(): return (summed / (1.0 + jnp.exp(-summed))).astype(jnp.bfloat16)]
where the time goes in v4:
time: 44.7 us; the launch traced here: 44.2 us
  Pallas kernels  42.5 us (95%)
  other arithmetic  1.68 us (4%)
    pallas_call x1, Pallas kernels, per_device(): pl.pallas_call(functools.partial(layer_kernel, seq, chan, each, parts, to...  42.5 us
    convert_element_type x1, other arithmetic, per_device(): return (summed / (1.0 + jnp.exp(-summed))).astype(jnp.bfloat16)  1.68 us

profile of v4, /device:TPU:0, one launch (start us, length us, event | category | flops | bytes accessed | tf_op | source)
XLA Modules:
  0.0 44.2 jit_solution(6788049659489199388)
XLA Ops:
  0.0 42.5 %shard_map.82 = f32[128,512]{1,0:T(8,128)} custom-call(bf16[16,8,512]{2,1,0:T(8,128)(2,1)} %bitcast.9, bf16[16,8,512]{2,1,0:T(8,128)(2,1)} %bitcast.10, bf16[16,8,512]{2,1,0:T(8,128)(2,1)} %bitcast.11, f32[16,8,512]{2,1,0:T(8,128)} %bitcast.7, f32[16,8,512]{2,1,0:T(8,128)} %bitcast.8, f32[1,128]{1,0:T(1,128)} %bitcast.12, f32[1,128]{1,0:T(1,128)} %bitcast.13, ...), custom_call_target="tpu_custom_call" | custom-call | tf_op jit(solution)/shard_map/pallas_call | solution.py:281
  42.5 1.7 %divide_convert_fusion = bf16[128,512]{1,0:T(8,128)(2,1)} fusion(f32[128,512]{1,0:T(8,128)} %shard_map.82), kind=kLoop, calls=%fused_computation | loop fusion | flops 262144 | bytes 393216 | tf_op jit(solution)/shard_map/convert_element_type | solution.py:309

commit v5 on v4

--- a/solution.py
+++ b/solution.py
@@ -10,7 +10,7 @@
 
 LANES = 128
 GROUP = 64
-PARTS = 1
+PARTS = 2
 MESH = pl.DeviceIdType.MESH
 
 
@@ -73,21 +73,24 @@
     pieces = (values, taps_one, gate_one, taps_two, gate_two)
     early, late = (0, 1), (2, 3, 4)
 
-    def piece_copy(piece, peer, slot):
+    def rows(part):
+        return pl.ds(part * share, share)
+
+    def piece_copy(part, piece, peer, slot):
         return to_peer(
-            pieces[piece].at[peer], got.at[piece, slot],
-            sent_out.at[piece, peer], sent_in.at[piece, slot], peer,
+            pieces[piece].at[peer, rows(part)], got.at[piece, slot, rows(part)],
+            sent_out.at[part, piece, peer], sent_in.at[part, piece, slot], peer,
         )
 
     def back_copy(part, peer, slot):
         return to_peer(
-            ready.at[part, peer], full.at[mine, slot, part],
+            ready.at[peer, rows(part)], full.at[mine, slot, rows(part)],
             back_out.at[part, peer], back_in.at[part, slot], peer,
         )
 
     def pass_copy(part, slot, group, offset):
         return pltpu.make_async_remote_copy(
-            src_ref=full.at[group, slot, part], dst_ref=full.at[group, slot, part],
+            src_ref=full.at[group, slot, rows(part)], dst_ref=full.at[group, slot, rows(part)],
             send_sem=pass_out.at[part, offset, slot], recv_sem=pass_in.at[part, group, slot],
             device_id=(me, sibling(offset)), device_id_type=MESH,
         )
@@ -131,37 +134,38 @@
         for piece in early + late
     ]
     for group in (early, late):
-
-        def send(peer, group=group):
-            for piece in group:
-                piece_copy(piece, peer, me).start()
-
-        each_other(send)
-        for piece in group:
-            own_copies[piece].start()
+        for part in range(parts):
+
+            def send(peer, group=group, part=part):
+                for piece in group:
+                    piece_copy(part, piece, peer, me).start()
+
+            each_other(send)
+            if part == 0:
+                for piece in group:
+                    own_copies[piece].start()
     padded[pl.ds(0, lags), :] = jnp.zeros((lags, LANES), jnp.float32)
 
-    def lay_out(group):
+    def lay_out(group, part):
         def wait(peer):
             for piece in group:
-                piece_copy(piece, peer, peer).wait_recv()
+                piece_copy(part, piece, peer, peer).wait_recv()
 
         each_other(wait)
-        for piece in group:
-            own_copies[piece].wait()
+        if part == 0:
+            for piece in group:
+                own_copies[piece].wait()
 
         def step(source, carry):
             for piece in group:
-                block = got[piece, source].astype(jnp.float32)
                 for tile in range(tiles):
-                    lines[piece, rows_of(source * tiles + tile, each, lags), :] = block[
-                        :, tile * LANES : (tile + 1) * LANES
-                    ]
+                    block = got[piece, source, rows(part), pl.ds(tile * LANES, LANES)]
+                    lines[
+                        piece, rows_of(part * share * lags + source * tiles + tile, share, lags), :
+                    ] = block.astype(jnp.float32)
             return carry
 
         lax.fori_loop(0, seq, step, 0)
-
-    lay_out(early)
 
     def first_conv(channel, carry):
         base = pl.multiple_of(channel * lags, lags)
@@ -169,9 +173,9 @@
         lines[0, pl.ds(base, lags), :] = toeplitz_conv(padded, lines.at[1, pl.ds(base, lags)], lags)
         return carry
 
-    lax.fori_loop(0, each, first_conv, 0)
-
-    lay_out(late)
+    for part in range(parts):
+        lay_out(early, part)
+        lax.fori_loop(part * share, (part + 1) * share, first_conv, 0)
 
     def second_conv(channel, carry):
         base = pl.multiple_of(channel * lags, lags)
@@ -183,11 +187,12 @@
 
     own_back = []
     for part in range(parts):
+        lay_out(late, part)
         lax.fori_loop(part * share, (part + 1) * share, second_conv, 0)
 
         def gather(target, carry, part=part):
             for tile in range(tiles):
-                ready[part, target, :, pl.ds(tile * LANES, LANES)] = lines[
+                ready[target, rows(part), pl.ds(tile * LANES, LANES)] = lines[
                     0, rows_of(part * share * lags + target * tiles + tile, share, lags), :
                 ].astype(ready.dtype)
             return carry
@@ -195,7 +200,9 @@
         lax.fori_loop(0, seq, gather, 0)
         each_other(lambda peer, part=part: back_copy(part, peer, me).start())
         own_back.append(
-            pltpu.make_async_copy(ready.at[part, me], full.at[mine, me, part], own.at[len(pieces) + part])
+            pltpu.make_async_copy(
+                ready.at[me, rows(part)], full.at[mine, me, rows(part)], own.at[len(pieces) + part]
+            )
         )
         own_back[-1].start()
 
@@ -214,10 +221,7 @@
         each_other(arrived)
 
     def widen(group, slot):
-        for part in range(parts):
-            wide[pl.ds((group * seq + slot) * each + part * share, share), :] = full[
-                group, slot, part
-            ].astype(jnp.float32)
+        wide[pl.ds((group * seq + slot) * each, each), :] = full[group, slot].astype(jnp.float32)
 
     def widen_mine(slot, carry):
         widen(mine, slot)
@@ -242,9 +246,11 @@
         preferred_element_type=jnp.float32,
     )
 
-    for piece in early + late:
-        each_other(lambda peer, piece=piece: piece_copy(piece, peer, me).wait_send())
     for part in range(parts):
+        for piece in early + late:
+            each_other(
+                lambda peer, piece=piece, part=part: piece_copy(part, piece, peer, me).wait_send()
+            )
         each_other(lambda peer, part=part: back_copy(part, peer, me).wait_send())
         for offset in range(1, chan):
 
@@ -277,7 +283,6 @@
     anywhere = pl.BlockSpec(memory_space=pl.ANY)
     vmem = pl.BlockSpec(memory_space=pltpu.VMEM)
     dma = pltpu.SemaphoreType.DMA
-    share = each // parts
     summed = pl.pallas_call(
         functools.partial(layer_kernel, seq, chan, each, parts, tokens),
         in_specs=[anywhere] * 3 + [vmem] * 5,
@@ -290,11 +295,11 @@
             pltpu.VMEM((5, seq, each, tokens), jnp.bfloat16),
             pltpu.VMEM((5, each * lags, LANES), jnp.float32),
             pltpu.VMEM((2 * lags, LANES), jnp.float32),
-            pltpu.VMEM((parts, seq, share, tokens), jnp.bfloat16),
-            pltpu.VMEM((chan, seq, parts, share, tokens), jnp.bfloat16),
+            pltpu.VMEM((seq, each, tokens), jnp.bfloat16),
+            pltpu.VMEM((chan, seq, each, tokens), jnp.bfloat16),
             pltpu.VMEM((chan * room, tokens), jnp.float32),
-            dma((5, seq)),
-            dma((5, seq)),
+            dma((parts, 5, seq)),
+            dma((parts, 5, seq)),
             dma((parts, seq)),
             dma((parts, seq)),
             dma((parts, chan, seq)),

time: 44.7 us -> 46 us (1.029)
  Pallas kernels: 42.5 us -> 43.8 us
    pallas_call x1, Pallas kernels: 42.5 us -> 43.8 us  [per_device(): pl.pallas_call(functools.partial(layer_kernel, seq, chan, each, parts, to...]
where the time goes in v5:
time: 46 us; the launch traced here: 45.5 us
  Pallas kernels  43.8 us (95%)
  other arithmetic  1.68 us (4%)
    pallas_call x1, Pallas kernels, per_device(): pl.pallas_call(functools.partial(layer_kernel, seq, chan, each, parts, to...  43.8 us
    convert_element_type x1, other arithmetic, per_device(): return (summed / (1.0 + jnp.exp(-summed))).astype(jnp.bfloat16)  1.68 us

profile of v5, /device:TPU:0, one launch (start us, length us, event | category | flops | bytes accessed | tf_op | source)
XLA Modules:
  0.0 45.5 jit_solution(2663599635120507618)
XLA Ops:
  0.0 43.8 %shard_map.82 = f32[128,512]{1,0:T(8,128)} custom-call(bf16[16,8,512]{2,1,0:T(8,128)(2,1)} %bitcast.9, bf16[16,8,512]{2,1,0:T(8,128)(2,1)} %bitcast.10, bf16[16,8,512]{2,1,0:T(8,128)(2,1)} %bitcast.11, f32[16,8,512]{2,1,0:T(8,128)} %bitcast.7, f32[16,8,512]{2,1,0:T(8,128)} %bitcast.8, f32[1,128]{1,0:T(1,128)} %bitcast.12, f32[1,128]{1,0:T(1,128)} %bitcast.13, ...), custom_call_target="tpu_custom_call" | custom-call | tf_op jit(solution)/shard_map/pallas_call | solution.py:286
  43.8 1.7 %divide_convert_fusion = bf16[128,512]{1,0:T(8,128)(2,1)} fusion(f32[128,512]{1,0:T(8,128)} %shard_map.82), kind=kLoop, calls=%fused_computation | loop fusion | flops 262144 | bytes 393216 | tf_op jit(solution)/shard_map/convert_element_type | solution.py:314

commit v6 on v5

--- a/solution.py
+++ b/solution.py
@@ -10,7 +10,7 @@
 
 LANES = 128
 GROUP = 64
-PARTS = 2
+PARTS = 1
 MESH = pl.DeviceIdType.MESH
 
 
@@ -50,7 +50,7 @@
 def layer_kernel(
     seq, chan, each, parts, tokens,
     values, gate_one, gate_two, filter_one, filter_two, skip_one, skip_two, mix, out,
-    taps_one, taps_two, direct, got, lines, padded, ready, full, wide,
+    boxes_early, boxes_late, got_early, got_late, direct, lines, padded, ready, full, wide,
     sent_out, sent_in, back_out, back_in, pass_out, pass_in, own,
 ):
     me, mine = lax.axis_index("seq"), lax.axis_index("chan")
@@ -70,16 +70,15 @@
             device_id=(peer, mine), device_id_type=MESH,
         )
 
-    pieces = (values, taps_one, gate_one, taps_two, gate_two)
-    early, late = (0, 1), (2, 3, 4)
+    boxes, got = (boxes_early, boxes_late), (got_early, got_late)
 
     def rows(part):
         return pl.ds(part * share, share)
 
-    def piece_copy(part, piece, peer, slot):
+    def box_copy(group, peer, slot):
         return to_peer(
-            pieces[piece].at[peer, rows(part)], got.at[piece, slot, rows(part)],
-            sent_out.at[part, piece, peer], sent_in.at[part, piece, slot], peer,
+            boxes[group].at[peer], got[group].at[slot],
+            sent_out.at[group, peer], sent_in.at[group, slot], peer,
         )
 
     def back_copy(part, peer, slot):
@@ -109,7 +108,22 @@
     for offset in range(1, chan):
         pl.semaphore_signal(barrier, inc=1, device_id=(me, sibling(offset)), device_id_type=MESH)
     room = seq * each
-    for taps, source, skip in ((taps_one, filter_one, skip_one), (taps_two, filter_two, skip_two)):
+    packed = [
+        pltpu.make_async_copy(source, box, own.at[index])
+        for index, (source, box) in enumerate(
+            (
+                (values, boxes_early.at[:, 0]),
+                (gate_one, boxes_late.at[:, 0]),
+                (gate_two, boxes_late.at[:, 1]),
+            )
+        )
+    ]
+    for copy in packed:
+        copy.start()
+    for taps, place, source, skip in (
+        (boxes_early, 1, filter_one, skip_one),
+        (boxes_late, 2, filter_two, skip_two),
+    ):
         row = lax.broadcasted_iota(jnp.int32, (room, room), 0)
         lane = lax.broadcasted_iota(jnp.int32, (room, room), 1)
         column = jnp.sum(
@@ -118,51 +132,41 @@
         lane = lax.broadcasted_iota(jnp.int32, (room, LANES), 1)
         direct[...] = jnp.where(lane + me == 0, column, 0.0)
 
-        def make_taps(target, carry, taps=taps, source=source):
+        def make_taps(target, carry, taps=taps, place=place, source=source):
             for tile in range(tiles):
                 part = source[target, :, pl.ds(tile * LANES, LANES)]
                 if tile == 0:
                     part = part + direct[pl.ds(target * each, each), :]
-                taps[target, :, pl.ds(tile * LANES, LANES)] = part.astype(taps.dtype)
+                taps[target, place, :, pl.ds(tile * LANES, LANES)] = part.astype(taps.dtype)
             return carry
 
         lax.fori_loop(0, seq, make_taps, 0)
     pl.semaphore_wait(barrier, seq - 1 + chan - 1)
 
     own_copies = [
-        pltpu.make_async_copy(pieces[piece].at[me], got.at[piece, me], own.at[piece])
-        for piece in early + late
+        pltpu.make_async_copy(boxes[group].at[me], got[group].at[me], own.at[3 + group])
+        for group in range(2)
     ]
-    for group in (early, late):
-        for part in range(parts):
-
-            def send(peer, group=group, part=part):
-                for piece in group:
-                    piece_copy(part, piece, peer, me).start()
-
-            each_other(send)
-            if part == 0:
-                for piece in group:
-                    own_copies[piece].start()
+    packed[0].wait()
+    each_other(lambda peer: box_copy(0, peer, me).start())
+    own_copies[0].start()
+    packed[1].wait()
+    packed[2].wait()
+    each_other(lambda peer: box_copy(1, peer, me).start())
+    own_copies[1].start()
     padded[pl.ds(0, lags), :] = jnp.zeros((lags, LANES), jnp.float32)
 
-    def lay_out(group, part):
-        def wait(peer):
-            for piece in group:
-                piece_copy(part, piece, peer, peer).wait_recv()
-
-        each_other(wait)
-        if part == 0:
-            for piece in group:
-                own_copies[piece].wait()
+    def lay_out(group, first):
+        each_other(lambda peer: box_copy(group, peer, peer).wait_recv())
+        own_copies[group].wait()
 
         def step(source, carry):
-            for piece in group:
+            for index in range(got[group].shape[1]):
+                block = got[group][source, index].astype(jnp.float32)
                 for tile in range(tiles):
-                    block = got[piece, source, rows(part), pl.ds(tile * LANES, LANES)]
-                    lines[
-                        piece, rows_of(part * share * lags + source * tiles + tile, share, lags), :
-                    ] = block.astype(jnp.float32)
+                    lines[first + index, rows_of(source * tiles + tile, each, lags), :] = block[
+                        :, tile * LANES : (tile + 1) * LANES
+                    ]
             return carry
 
         lax.fori_loop(0, seq, step, 0)
@@ -173,21 +177,20 @@
         lines[0, pl.ds(base, lags), :] = toeplitz_conv(padded, lines.at[1, pl.ds(base, lags)], lags)
         return carry
 
-    for part in range(parts):
-        lay_out(early, part)
-        lax.fori_loop(part * share, (part + 1) * share, first_conv, 0)
+    lay_out(0, 0)
+    lax.fori_loop(0, each, first_conv, 0)
+    lay_out(1, 2)
 
     def second_conv(channel, carry):
         base = pl.multiple_of(channel * lags, lags)
         here = pl.ds(base, lags)
         padded[pl.ds(lags, lags), :] = lines[2, here, :] * lines[0, here, :]
-        second = toeplitz_conv(padded, lines.at[3, here], lags)
-        lines[0, here, :] = lines[4, here, :] * second
+        second = toeplitz_conv(padded, lines.at[4, here], lags)
+        lines[0, here, :] = lines[3, here, :] * second
         return carry
 
     own_back = []
     for part in range(parts):
-        lay_out(late, part)
         lax.fori_loop(part * share, (part + 1) * share, second_conv, 0)
 
         def gather(target, carry, part=part):
@@ -201,7 +204,7 @@
         each_other(lambda peer, part=part: back_copy(part, peer, me).start())
         own_back.append(
             pltpu.make_async_copy(
-                ready.at[me, rows(part)], full.at[mine, me, rows(part)], own.at[len(pieces) + part]
+                ready.at[me, rows(part)], full.at[mine, me, rows(part)], own.at[5 + part]
             )
         )
         own_back[-1].start()
@@ -246,11 +249,9 @@
         preferred_element_type=jnp.float32,
     )
 
+    for group in range(2):
+        each_other(lambda peer, group=group: box_copy(group, peer, me).wait_send())
     for part in range(parts):
-        for piece in early + late:
-            each_other(
-                lambda peer, piece=piece, part=part: piece_copy(part, piece, peer, me).wait_send()
-            )
         each_other(lambda peer, part=part: back_copy(part, peer, me).wait_send())
         for offset in range(1, chan):
 
@@ -289,17 +290,18 @@
         out_specs=vmem,
         out_shape=jax.ShapeDtypeStruct((made, tokens), jnp.float32),
         scratch_shapes=[
-            pltpu.VMEM((seq, each, tokens), jnp.bfloat16),
-            pltpu.VMEM((seq, each, tokens), jnp.bfloat16),
+            pltpu.VMEM((seq, 2, each, tokens), jnp.bfloat16),
+            pltpu.VMEM((seq, 3, each, tokens), jnp.bfloat16),
+            pltpu.VMEM((seq, 2, each, tokens), jnp.bfloat16),
+            pltpu.VMEM((seq, 3, each, tokens), jnp.bfloat16),
             pltpu.VMEM((room, LANES), jnp.float32),
-            pltpu.VMEM((5, seq, each, tokens), jnp.bfloat16),
             pltpu.VMEM((5, each * lags, LANES), jnp.float32),
             pltpu.VMEM((2 * lags, LANES), jnp.float32),
             pltpu.VMEM((seq, each, tokens), jnp.bfloat16),
             pltpu.VMEM((chan, seq, each, tokens), jnp.bfloat16),
             pltpu.VMEM((chan * room, tokens), jnp.float32),
-            dma((parts, 5, seq)),
-            dma((parts, 5, seq)),
+            dma((2, seq)),
+            dma((2, seq)),
             dma((parts, seq)),
             dma((parts, seq)),
             dma((parts, chan, seq)),

time: 46 us -> 42.7 us (0.928)
  Pallas kernels: 43.8 us -> 40.4 us
    pallas_call x1, Pallas kernels: 43.8 us -> 40.4 us  [per_device(): pl.pallas_call(functools.partial(layer_kernel, seq, chan, each, parts, to...]
where the time goes in v6:
time: 42.7 us; the launch traced here: 42.1 us
  Pallas kernels  40.4 us (95%)
  other arithmetic  1.68 us (4%)
    pallas_call x1, Pallas kernels, per_device(): pl.pallas_call(functools.partial(layer_kernel, seq, chan, each, parts, to...  40.4 us
    convert_element_type x1, other arithmetic, per_device(): return (summed / (1.0 + jnp.exp(-summed))).astype(jnp.bfloat16)  1.68 us

profile of v6, /device:TPU:0, one launch (start us, length us, event | category | flops | bytes accessed | tf_op | source)
XLA Modules:
  0.0 42.1 jit_solution(12797465851966120986)
XLA Ops:
  0.0 40.4 %shard_map.82 = f32[128,512]{1,0:T(8,128)} custom-call(bf16[16,8,512]{2,1,0:T(8,128)(2,1)} %bitcast.9, bf16[16,8,512]{2,1,0:T(8,128)(2,1)} %bitcast.10, bf16[16,8,512]{2,1,0:T(8,128)(2,1)} %bitcast.11, f32[16,8,512]{2,1,0:T(8,128)} %bitcast.7, f32[16,8,512]{2,1,0:T(8,128)} %bitcast.8, f32[1,128]{1,0:T(1,128)} %bitcast.12, f32[1,128]{1,0:T(1,128)} %bitcast.13, ...), custom_call_target="tpu_custom_call" | custom-call | tf_op jit(solution)/shard_map/pallas_call | solution.py:287
  40.4 1.7 %divide_convert_fusion = bf16[128,512]{1,0:T(8,128)(2,1)} fusion(f32[128,512]{1,0:T(8,128)} %shard_map.82), kind=kLoop, calls=%fused_computation | loop fusion | flops 262144 | bytes 393216 | tf_op jit(solution)/shard_map/convert_element_type | solution.py:316

commit v7 on v6

--- a/solution.py
+++ b/solution.py
@@ -87,10 +87,10 @@
             back_out.at[part, peer], back_in.at[part, slot], peer,
         )
 
-    def pass_copy(part, slot, group, offset):
+    def pass_copy(group, offset):
         return pltpu.make_async_remote_copy(
-            src_ref=full.at[group, slot, rows(part)], dst_ref=full.at[group, slot, rows(part)],
-            send_sem=pass_out.at[part, offset, slot], recv_sem=pass_in.at[part, group, slot],
+            src_ref=full.at[group], dst_ref=full.at[group],
+            send_sem=pass_out.at[offset], recv_sem=pass_in.at[group],
             device_id=(me, sibling(offset)), device_id_type=MESH,
         )
 
@@ -209,19 +209,11 @@
         )
         own_back[-1].start()
 
-    def pass_on(part, slot):
-        for offset in range(1, chan):
-            pass_copy(part, slot, mine, offset).start()
-
     for part in range(parts):
         own_back[part].wait()
-        pass_on(part, me)
-
-        def arrived(peer, part=part):
-            back_copy(part, peer, peer).wait_recv()
-            pass_on(part, peer)
-
-        each_other(arrived)
+        each_other(lambda peer, part=part: back_copy(part, peer, peer).wait_recv())
+    for offset in range(1, chan):
+        pass_copy(mine, offset).start()
 
     def widen(group, slot):
         wide[pl.ds((group * seq + slot) * each, each), :] = full[group, slot].astype(jnp.float32)
@@ -233,10 +225,9 @@
     lax.fori_loop(0, seq, widen_mine, 0)
     for offset in range(1, chan):
         group = sibling(offset)
+        pass_copy(group, offset).wait_recv()
 
         def widen_other(slot, carry, group=group, offset=offset):
-            for part in range(parts):
-                pass_copy(part, slot, group, offset).wait_recv()
             widen(group, slot)
             return carry
 
@@ -253,13 +244,8 @@
         each_other(lambda peer, group=group: box_copy(group, peer, me).wait_send())
     for part in range(parts):
         each_other(lambda peer, part=part: back_copy(part, peer, me).wait_send())
-        for offset in range(1, chan):
-
-            def sent(slot, carry, part=part, offset=offset):
-                pass_copy(part, slot, mine, offset).wait_send()
-                return carry
-
-            lax.fori_loop(0, seq, sent, 0)
+    for offset in range(1, chan):
+        pass_copy(mine, offset).wait_send()
 
 
 def per_device(
@@ -304,8 +290,8 @@
             dma((2, seq)),
             dma((parts, seq)),
             dma((parts, seq)),
-            dma((parts, chan, seq)),
-            dma((parts, chan, seq)),
+            dma((chan,)),
+            dma((chan,)),
             dma((5 + parts,)),
         ],
         compiler_params=pltpu.CompilerParams(collective_id=0, has_side_effects=True),

time: 42.7 us -> 42.3 us (level)
  Pallas kernels: 40.4 us -> 39.8 us
    pallas_call x1, Pallas kernels: 40.4 us -> 39.8 us  [per_device(): pl.pallas_call(functools.partial(layer_kernel, seq, chan, each, parts, to...]
where the time goes in v7:
time: 42.3 us; the launch traced here: 41.5 us
  Pallas kernels  39.8 us (94%)
  other arithmetic  1.68 us (4%)
    pallas_call x1, Pallas kernels, per_device(): pl.pallas_call(functools.partial(layer_kernel, seq, chan, each, parts, to...  39.8 us
    convert_element_type x1, other arithmetic, per_device(): return (summed / (1.0 + jnp.exp(-summed))).astype(jnp.bfloat16)  1.68 us

profile of v7, /device:TPU:0, one launch (start us, length us, event | category | flops | bytes accessed | tf_op | source)
XLA Modules:
  0.0 41.5 jit_solution(14819407001027717931)
XLA Ops:
  0.0 39.8 %shard_map.82 = f32[128,512]{1,0:T(8,128)} custom-call(bf16[16,8,512]{2,1,0:T(8,128)(2,1)} %bitcast.9, bf16[16,8,512]{2,1,0:T(8,128)(2,1)} %bitcast.10, bf16[16,8,512]{2,1,0:T(8,128)(2,1)} %bitcast.11, f32[16,8,512]{2,1,0:T(8,128)} %bitcast.7, f32[16,8,512]{2,1,0:T(8,128)} %bitcast.8, f32[1,128]{1,0:T(1,128)} %bitcast.12, f32[1,128]{1,0:T(1,128)} %bitcast.13, ...), custom_call_target="tpu_custom_call" | custom-call | tf_op jit(solution)/shard_map/pallas_call | solution.py:273
  39.8 1.7 %divide_convert_fusion = bf16[128,512]{1,0:T(8,128)(2,1)} fusion(f32[128,512]{1,0:T(8,128)} %shard_map.82), kind=kLoop, calls=%fused_computation | loop fusion | flops 262144 | bytes 393216 | tf_op jit(solution)/shard_map/convert_element_type | solution.py:302
